TPU v7x, 32 devices: a whole 2x2x4 slice. The times are simulated.
32 devices in a mesh: group: 2 (over x), box: 8 (over z, y), sample: 2 (over core).
Axes of the slice: x: 2, y: 2, z: 4, core: 2. Of those that a mesh axis runs over, the one named last changes fastest.
Arguments:
- krylov: float32 [2, 4, 4, 96, 256], P(None, None, None, ('group', 'box', 'sample')), parts along dimension 3, as said below
- self_inv: bfloat16 [2, 96, 256, 256], P(None, ('group', 'box', 'sample')), parts along dimension 1
- node_pos: float32 [3, 96, 256], P(None, ('group', 'box', 'sample')), parts along dimension 1, as said below
- node_wts: float32 [96, 256], P(('group', 'box', 'sample')), parts along dimension 0, may hold values from 0.02 to 0.2
- box_of: int32 [96], P(('group', 'box', 'sample')), parts along dimension 0, may hold values from 0 to 31, as said below
- near_list: int32 [96, 4], P(('group', 'box', 'sample')), parts along dimension 0, may hold values from 0 to 47, as said below
- leaf_src: int32 [64, 4], P(('group', 'box', 'sample')), parts along dimension 0, may hold values from 0 to 31, as said below
- leaf_op: int32 [64, 4], P(('group', 'box', 'sample')), parts along dimension 0, may hold values from 0 to 159
- leaf_ops: float32 [160, 2, 512], replicated, may hold values from -5 to 5
- interp: float32 [512, 2048], replicated, may hold values from -0.25 to 0.25
- parent_centers: float32 [3, 16], P(None, ('group', 'box')), parts along dimension 1
- up_src: int32 [16, 6], P('group'), parts along dimension 0, may hold values from 0 to 7, as said below
- up_op: int32 [16, 6], P('group'), parts along dimension 0, may hold values from 0 to 159
- up_ops: float32 [160, 2, 2048], P(None, None, 'sample'), may hold values from -1.5 to 1.5
Outputs:
- h_column: float32 [2, 4, 8], P(None, None, 'group'), parts along dimension 2
- h_norm: float32 [8], P('group'), parts along dimension 0
- next_vector: float32 [2, 4, 48, 512], P(None, None, ('box', 'sample'), 'group'), parts along dimension 3
There are 2 independent parts, one for each index of `group`. A program takes and returns all parts, laid end to end along the dimension named above; an argument that names none is the same for every part. Nothing has to cross between parts.
Inputs may be any that keep to these rules, and one draw needn't show every extreme that they name: `krylov`: for each incidence the 4 vectors are orthonormal under the inner product that is the mean of conj(a) b over all nodes. `box_of`: Non-decreasing; ellipsoid e lies in one of the boxes 2 * (e // 3) to 2 * (e // 3) + 1, each of which holds at least one ellipsoid. `near_list`: an entry of row e is another ellipsoid at most 3 indices away from e. `leaf_src`: an entry of row b is another leaf box at most 2 indices away from b. `up_src`: no row names its own coarse box. `node_pos`: nodes of different ellipsoids are at least 0.2 apart.
All inputs are finite; a program needn't handle non-finite values.
Results may differ from a plain program's by a relative error of at most 0.0034.
Values sent between devices are 32-bit elements; how exact they have to be, the bound alone decides.
A program may use at most 64 MiB of HBM per device.

v0:
```python
import functools
import math

import jax
import jax.numpy as jnp
import numpy as np
from jax import lax
from jax.experimental import pallas as pl
from jax.experimental.pallas import tpu as pltpu
from jax.sharding import PartitionSpec as P

MESH = pl.DeviceIdType.MESH
F32 = jnp.float32
BF16 = jnp.bfloat16
ROWS = 64


def sphere_points(total):
    position = np.arange(total).astype(np.float32)
    height = np.float32(1.0) - (np.float32(2.0) * position + np.float32(1.0)) / np.float32(total)
    radius = np.sqrt(np.float32(1.0) - height * height)
    angle = (position * np.float32(math.pi * (3.0 - math.sqrt(5.0)))).astype(np.float64)
    points = [radius * np.cos(angle).astype(np.float32), radius * np.sin(angle).astype(np.float32), height]
    return np.stack(points).astype(np.float32)


SIN_COEFS = (6.283185280261419, -10.335420167015924, 5.100155046431118, -1.1965825712511455, 0.15531532062982073)
COS_COEFS = (0.9999999532476092, -4.9347928306196795, 4.058411352863147, -1.3318765680841478, 0.21968961110420304)


def turn(t):
    f = t - jnp.floor(t + 0.5)
    u = f * f
    s = SIN_COEFS[-1]
    for coef in SIN_COEFS[-2::-1]:
        s = s * u + coef
    s = s * f
    c = COS_COEFS[-1]
    for coef in COS_COEFS[-2::-1]:
        c = c * u + coef
    return 1.0 - 0.5 * s * s, s * c


def pair(x):
    high = x.astype(BF16).astype(F32)
    return jnp.concatenate([high, x - high], axis=0).astype(BF16)


def both(x, table, contract):
    rows = x.shape[0]
    out = lax.dot_general(
        pair(x), table, (((1,), (contract,)), ((), ())), preferred_element_type=F32
    )
    return out[:rows] + out[rows:]


def kernel(
    box_count_axis,
    sample_count_axis,
    box_of_hbm,
    near_list_hbm,
    leaf_src_hbm,
    leaf_op_hbm,
    up_src_hbm,
    up_op_hbm,
    parent_centers_hbm,
    krylov_hbm,
    self_inv_hbm,
    node_pos_hbm,
    node_wts_hbm,
    leaf_dirs_hbm,
    up_dirs_hbm,
    leaf_ops_hbm,
    interp_hbm,
    up_ops_hbm,
    h_out,
    norm_out,
    next_out,
    box_of,
    near_list,
    leaf_src,
    leaf_op,
    up_src,
    up_op,
    parent_centers,
    krylov,
    self_inv,
    node_pos,
    node_wts,
    leaf_dirs,
    up_dirs,
    leaf_ops,
    interp_raw,
    up_ops,
    interp,
    ks,
    halo,
    shifted,
    columns,
    cos_tab,
    sin_tab,
    pat,
    gathered,
    full,
    near_r,
    near_i,
    near_acc,
    result,
    sums,
    local_sem,
    send_a,
    recv_a,
    send_b,
    recv_b,
    send_c,
    recv_c,
    send_d,
    recv_d,
    send_e,
    recv_e,
):
    nb, ns = box_count_axis, sample_count_axis
    nd = nb * ns
    _, vectors, ells, inc, nodes = krylov.shape
    rows = 2 * inc
    boxes = leaf_src.shape[0]
    near_count = near_list.shape[1]
    leaf_width = interp.shape[1]
    half = interp.shape[2]
    bi = lax.axis_index("box")
    si = lax.axis_index("sample")
    dev = bi * ns + si

    def load(slot, source, target):
        copy = pltpu.make_async_copy(source, target, local_sem.at[slot])
        copy.start()
        return copy

    loads = {}
    arrays = dict(
        node_pos=(node_pos_hbm, node_pos), box_of=(box_of_hbm, box_of), leaf_dirs=(leaf_dirs_hbm, leaf_dirs),
        krylov=(krylov_hbm, krylov), node_wts=(node_wts_hbm, node_wts), self_inv=(self_inv_hbm, self_inv),
        parent_centers=(parent_centers_hbm, parent_centers), up_dirs=(up_dirs_hbm, up_dirs),
        near_list=(near_list_hbm, near_list), leaf_src=(leaf_src_hbm, leaf_src), leaf_op=(leaf_op_hbm, leaf_op),
        up_src=(up_src_hbm, up_src), up_op=(up_op_hbm, up_op),
    )
    for name, (source, target) in arrays.items():
        loads[name] = load(len(loads), source, target)
    for h in range(ns):
        loads["interp", h] = load(len(loads), interp_hbm.at[:, pl.ds(h * half, half)], interp_raw.at[h])
    loads["up_ops"] = load(len(loads), up_ops_hbm, up_ops)
    loads["leaf_ops"] = load(len(loads), leaf_ops_hbm, leaf_ops)

    def ready(*wanted):
        for name in wanted:
            loads[name].wait()

    def place(index):
        return {"box": index // ns, "sample": index % ns}

    barrier = pltpu.get_barrier_semaphore()
    for off in range(1, nd):
        pl.semaphore_signal(barrier, inc=1, device_id=place((dev + off) % nd), device_id_type=MESH)

    sign = jnp.where(lax.broadcasted_iota(jnp.int32, (rows, 1), 0) < inc, 1.0, -1.0)

    def swap(x):
        return pltpu.roll(x, inc, 0)

    def inward(c, d):
        return c - sign * swap(d)

    def outward(c, d):
        return c + sign * swap(d)

    def neighbours(buffer, width, send, recv):
        own = buffer.at[pl.ds(width, width)]
        right = pltpu.make_async_remote_copy(
            src_ref=own, dst_ref=buffer.at[pl.ds(0, width)], send_sem=send.at[0], recv_sem=recv.at[0],
            device_id=place((dev + 1) % nd), device_id_type=MESH,
        )
        left = pltpu.make_async_remote_copy(
            src_ref=own, dst_ref=buffer.at[pl.ds(2 * width, width)], send_sem=send.at[1], recv_sem=recv.at[1],
            device_id=place((dev + nd - 1) % nd), device_id_type=MESH,
        )

        def start():
            @pl.when(dev < nd - 1)
            def _():
                right.start()

            @pl.when(dev > 0)
            def _():
                left.start()

        def arrive():
            @pl.when(dev > 0)
            def _():
                right.wait_recv()

            @pl.when(dev < nd - 1)
            def _():
                left.wait_recv()

        def finish():
            @pl.when(dev < nd - 1)
            def _():
                right.wait_send()

            @pl.when(dev > 0)
            def _():
                left.wait_send()

        return start, arrive, finish

    start_a, arrive_a, finish_a = neighbours(halo, ells, send_a, recv_a)
    start_b, arrive_b, finish_b = neighbours(pat, boxes, send_b, recv_b)

    ready("node_pos", "box_of", "leaf_dirs")
    for e in range(ells):
        for axis in range(3):
            halo[ells + e, rows + axis : rows + axis + 1, :] = node_pos[axis, e : e + 1, :]
        halo[ells + e, rows + 3 :, :] = jnp.zeros((halo.shape[1] - rows - 3, nodes), F32)

    member = [
        [jnp.where(box_of[e] - dev * boxes == b, 1.0, 0.0) for e in range(ells)] for b in range(boxes)
    ]
    position_sum = [
        jnp.sum(halo[ells + e, rows : rows + 8, :], axis=1, keepdims=True) for e in range(ells)
    ]
    centers = []
    for b in range(boxes):
        total = position_sum[0] * member[b][0]
        amount = member[b][0]
        for e in range(1, ells):
            total = total + position_sum[e] * member[b][e]
            amount = amount + member[b][e]
        centers.append(total / (jnp.full((8, 1), 1.0, F32) * (amount * nodes)))
    for e in range(ells):
        middle = centers[0] * member[0][e]
        for b in range(1, boxes):
            middle = middle + centers[b] * member[b][e]
        here = halo[ells + e, rows : rows + 8, :]
        shifted[e] = here - middle
        columns[e] = jnp.transpose(here)

    def fill(chunk, carry):
        at = pl.multiple_of(chunk * ROWS, ROWS)
        ways = [
            jnp.broadcast_to(leaf_dirs[pl.ds(at, ROWS), axis : axis + 1], (ROWS, nodes)) for axis in range(3)
        ]
        for e in range(ells):
            t = ways[0] * shifted[e, 0:1, :]
            for axis in range(1, 3):
                t = t + ways[axis] * shifted[e, axis : axis + 1, :]
            cosine, sine = turn(t)
            cos_tab[e, pl.ds(at, ROWS), :] = cosine.astype(BF16)
            sin_tab[e, pl.ds(at, ROWS), :] = sine.astype(BF16)
        return carry

    lax.fori_loop(0, leaf_width // ROWS, fill, 0)

    ready("krylov", "node_wts", "self_inv")
    for e in range(ells):
        for m in range(vectors):
            for q in range(2):
                ks[m, e, q * inc : (q + 1) * inc, :] = krylov[q, m, e]
    nt = (((1,), (1,)), ((), ()))
    for e in range(ells):
        rounded = ks[vectors - 1, e].astype(BF16)
        c = lax.dot_general(rounded, self_inv[0, e], nt, preferred_element_type=F32)
        d = lax.dot_general(rounded, self_inv[1, e], nt, preferred_element_type=F32)
        halo[ells + e, 0:rows, :] = inward(c, d) * node_wts[e : e + 1, :]

    radiated = []
    for e in range(ells):
        values = halo[ells + e, 0:rows, :]
        radiated.append(outward(both(values, cos_tab[e], 1), both(values, sin_tab[e], 1)))
    for b in range(boxes):
        total = radiated[0] * member[b][0]
        for e in range(1, ells):
            total = total + radiated[e] * member[b][e]
        pat[boxes + b, 0:rows, :] = total
        pat[boxes + b, rows:, :] = jnp.broadcast_to(centers[b], (8, leaf_width))
    pl.semaphore_wait(barrier, nd - 1)
    start_b()
    start_a()

    for h in range(ns):
        ready(("interp", h))

        def cast(chunk, carry, h=h):
            at = pl.multiple_of(chunk * 16, 16)
            interp[h, pl.ds(at, 16), :] = interp_raw[h, pl.ds(at, 16), :].astype(BF16)
            return carry

        lax.fori_loop(0, leaf_width // 16, cast, 0)

    def up_phase(center, dirs):
        t = (center[0:1] - parent_centers[0, 0]) * dirs[0:1]
        for axis in range(1, 3):
            t = t + (center[axis : axis + 1] - parent_centers[0, axis]) * dirs[axis : axis + 1]
        return t

    def turns_of(list_of_centers, dirs):
        return turn(jnp.concatenate([up_phase(center, dirs) for center in list_of_centers], axis=0))

    ready("parent_centers", "up_dirs")
    arrive_b()
    first = (1 - si) * boxes
    children = ns * boxes
    child_centers = [pat[first + c, rows:, 0:1] for c in range(children)]
    child_cos, child_sin = turns_of(child_centers, up_dirs[si])
    lifted = both(
        jnp.concatenate([pat[first + c, 0:rows, :] for c in range(children)], axis=0), interp[si], 0
    )
    parent = None
    for c in range(children):
        piece = lifted[c * rows : (c + 1) * rows]
        term = outward(piece * child_cos[c : c + 1], piece * child_sin[c : c + 1])
        parent = term if parent is None else parent + term
    gathered[bi] = parent

    twins = 2 if nb % 2 == 0 else 1
    levels = nb // twins
    level = bi // twins
    twin = level * twins + (bi + 1) % twins

    def hop(slot, way):
        target = (twin, (bi + twins) % nb, (bi + nb - twins) % nb)[way]
        return pltpu.make_async_remote_copy(
            src_ref=gathered.at[slot], dst_ref=gathered.at[slot], send_sem=send_c.at[slot, way],
            recv_sem=recv_c.at[slot], device_id={"box": target, "sample": si}, device_id_type=MESH,
        )

    def hand_over(slot, ways, act):
        if twins > 1:
            act(hop(slot, 0))
        for way in ways:
            room = level < levels - 1 if way == 1 else level > 0

            @pl.when(room)
            def _(way=way):
                act(hop(slot, way))

    def relay(distance, act, wait):
        for way, there, slot in (
            (1, level >= distance, bi - distance * twins),
            (2, level < levels - distance, bi + distance * twins),
        ):
            @pl.when(there)
            def _(way=way, slot=slot):
                if wait:
                    hop(slot, way).wait_recv()
                hand_over(slot, (way,), act)

    hand_over(bi, (1, 2), lambda copy: copy.start())

    def translate(operators, index, values):
        pair_rows = operators[index]
        return inward(values * pair_rows[0:1], values * pair_rows[1:2])

    ready("leaf_src", "leaf_op", "leaf_ops")
    incoming = []
    for b in range(boxes):
        total = None
        for j in range(leaf_src.shape[1]):
            source = pat[jnp.clip(leaf_src[b, j] - (dev - 1) * boxes, 0, 3 * boxes - 1)]
            term = translate(leaf_ops, leaf_op[b, j], source[0:rows])
            total = term if total is None else total + term
        incoming.append(total)

    halves = (si, (si + 1) % ns)
    own_phase = [turns_of(centers, up_dirs[h]) for h in halves]

    ready("near_list")
    arrive_a()
    near_acc[...] = jnp.zeros(near_acc.shape, F32)

    def near_pair(index, carry):
        e = index // near_count
        j = index % near_count
        source = halo[jnp.clip(near_list[e, j] - (dev - 1) * ells, 0, 3 * ells - 1)]
        for chunk in range(nodes // ROWS):
            target = columns[e, chunk * ROWS : (chunk + 1) * ROWS, :]
            squared = None
            for axis in range(3):
                gap = target[:, axis : axis + 1] - source[rows + axis : rows + axis + 1]
                squared = gap * gap if squared is None else squared + gap * gap
            inverse = lax.rsqrt(squared)
            cosine, sine = turn(squared * inverse)
            near_r[chunk * ROWS : (chunk + 1) * ROWS, :] = (cosine * inverse).astype(BF16)
            near_i[chunk * ROWS : (chunk + 1) * ROWS, :] = (sine * inverse).astype(BF16)
        values = source[0:rows]
        near_acc[e] += inward(both(values, near_r[...], 1), both(values, near_i[...], 1))
        return carry

    pairs_total = ells * near_count
    last = pairs_total - near_count // 2
    share = max(1, last // (levels + 1))
    done = 0
    for distance in range(1, levels):
        upto = min(done + share, last)
        if upto > done:
            lax.fori_loop(done, upto, near_pair, 0)
        done = upto
        relay(distance, lambda copy: copy.start(), True)
    if last > done:
        lax.fori_loop(done, last, near_pair, 0)
    done = last
    ready("up_src", "up_op", "up_ops")
    if twins > 1:
        for other in range(levels):
            hop(other * twins + (bi + 1) % twins, 0).wait_recv()
    parent_in = None
    for j in range(up_src.shape[1]):
        term = translate(up_ops, up_op[bi, j], gathered[up_src[bi, j]])
        parent_in = term if parent_in is None else parent_in + term
    full[si] = parent_in
    partner = pltpu.make_async_remote_copy(
        src_ref=full.at[si], dst_ref=full.at[si], send_sem=send_d.at[0], recv_sem=recv_d.at[0],
        device_id={"box": bi, "sample": (si + 1) % ns}, device_id_type=MESH,
    )
    partner.start()

    lax.fori_loop(done, pairs_total, near_pair, 0)
    def lower(h, phase):
        own_cos, own_sin = phase
        values = full[h]
        lowered = jnp.concatenate(
            [
                inward(values * own_cos[b : b + 1], values * own_sin[b : b + 1])
                for b in range(boxes)
            ],
            axis=0,
        )
        return both(lowered, interp[h], 1)

    lowered = lower(si, own_phase[0])
    partner.wait_recv()
    lowered = lowered + lower(halves[1], own_phase[1])
    for b in range(boxes):
        incoming[b] = incoming[b] + lowered[b * rows : (b + 1) * rows]

    lane = lax.broadcasted_iota(jnp.int32, (rows, 128), 1)
    row = lax.broadcasted_iota(jnp.int32, (rows, 128), 0)
    square = jnp.zeros((rows, 1), F32)
    straight = [jnp.zeros((rows, 1), F32) for _ in range(vectors)]
    crossed = [jnp.zeros((rows, 1), F32) for _ in range(vectors)]
    for e in range(ells):
        arriving = incoming[0] * member[0][e]
        for b in range(1, boxes):
            arriving = arriving + incoming[b] * member[b][e]
        far = inward(both(arriving, cos_tab[e], 0), both(arriving, sin_tab[e], 0))
        value = ks[vectors - 1, e] + near_acc[e] + far * leaf_width ** (-0.5)
        result[e] = value
        other = swap(value)
        square = square + jnp.sum(value * value, axis=1, keepdims=True)
        for m in range(vectors):
            basis = ks[m, e]
            straight[m] = straight[m] + jnp.sum(basis * value, axis=1, keepdims=True)
            crossed[m] = crossed[m] + jnp.sum(basis * other, axis=1, keepdims=True)
    packed = jnp.where(lane == vectors * rows + row, jnp.broadcast_to(square, lane.shape), 0.0)
    for m in range(vectors):
        a = jnp.broadcast_to(straight[m], lane.shape)
        b = jnp.broadcast_to(crossed[m], lane.shape)
        dots = jnp.where(row < inc, a + swap(a), swap(b) - b)
        packed = packed + jnp.where(lane == m * rows + row, dots, 0.0)
    sums[dev] = jnp.sum(packed, axis=0, keepdims=True)
    for off in range(1, nd):
        pltpu.make_async_remote_copy(
            src_ref=sums.at[dev], dst_ref=sums.at[dev], send_sem=send_e.at[off], recv_sem=recv_e.at[dev],
            device_id=place((dev + off) % nd), device_id_type=MESH,
        ).start()
    for off in range(1, nd):
        other = (dev + off) % nd
        pltpu.make_async_remote_copy(
            src_ref=sums.at[other], dst_ref=sums.at[other], send_sem=send_e.at[off],
            recv_sem=recv_e.at[other], device_id=place(other), device_id_type=MESH,
        ).wait_recv()
    total = sums[0]
    for index in range(1, nd):
        total = total + sums[index]
    total = total * (1.0 / (ells * nodes * nd))
    spread = jnp.broadcast_to(total, lane.shape)

    def column(start):
        return jnp.sum(
            jnp.where(lane == start + lax.rem(row, inc), spread, 0.0), axis=1, keepdims=True
        )

    real = [column(m * rows) for m in range(vectors)]
    imag = [column(m * rows + inc) for m in range(vectors)]
    norm_sq = column(vectors * rows) + column(vectors * rows + inc)
    for m in range(vectors):
        norm_sq = norm_sq - (real[m] * real[m] + imag[m] * imag[m])
    norm = jnp.sqrt(norm_sq)
    for m in range(vectors):
        for q in range(2):
            at = m * rows + q * inc
            h_out[q, m : m + 1, :] = total[:, at : at + inc]
    flat = jnp.sum(
        jnp.where((lane == row) & (row < inc), jnp.broadcast_to(norm, lane.shape), 0.0), axis=0, keepdims=True
    )
    norm_out[...] = flat[:, 0:inc]
    for e in range(ells):
        kept = result[e]
        for m in range(vectors):
            basis = ks[m, e]
            kept = kept - inward(basis * real[m], basis * imag[m])
        kept = kept / norm
        for q in range(2):
            next_out[q, e] = kept[q * inc : (q + 1) * inc]

    finish_a()
    finish_b()
    partner.wait_send()
    hand_over(bi, (1, 2), lambda copy: copy.wait_send())
    for distance in range(1, levels):
        relay(distance, lambda copy: copy.wait_send(), False)
    for off in range(1, nd):
        pltpu.make_async_remote_copy(
            src_ref=sums.at[dev], dst_ref=sums.at[dev], send_sem=send_e.at[off], recv_sem=recv_e.at[dev],
            device_id=place((dev + off) % nd), device_id_type=MESH,
        ).wait_send()


def hand_on(h_in, norm_in, next_in, h_out, norm_out, next_out):
    h_out[...] = h_in[...]
    norm_out[...] = norm_in[...]
    next_out[...] = next_in[...]


def body(
    nb,
    ns,
    krylov,
    self_inv,
    node_pos,
    node_wts,
    box_of,
    near_list,
    leaf_src,
    leaf_op,
    leaf_ops,
    interp,
    parent_centers,
    up_src,
    up_op,
    up_ops,
):
    _, vectors, inc, ells, nodes = krylov.shape
    rows = 2 * inc
    boxes = leaf_src.shape[0]
    leaf_width, up_width = interp.shape
    half = up_ops.shape[2]
    nd = nb * ns
    leaf_dirs = np.zeros((leaf_width, 8), np.float32)
    leaf_dirs[:, :3] = sphere_points(leaf_width).T
    up_dirs = np.zeros((ns, 8, half), np.float32)
    up_dirs[:, :3] = np.moveaxis(sphere_points(up_width).reshape(3, ns, half), 1, 0)
    small = [box_of, near_list, leaf_src, leaf_op, up_src, up_op, parent_centers.T]
    large = [jnp.transpose(krylov, (0, 1, 3, 2, 4)), self_inv, node_pos, node_wts]
    large += [jnp.asarray(leaf_dirs), jnp.asarray(up_dirs)]
    vmem = pl.BlockSpec(memory_space=pltpu.VMEM)
    hbm = pl.BlockSpec(memory_space=pl.ANY)
    dma = pltpu.SemaphoreType.DMA
    h_column, h_norm, next_vector = pl.pallas_call(
        functools.partial(kernel, nb, ns),
        out_shape=(
            jax.ShapeDtypeStruct((2, vectors, inc), F32),
            jax.ShapeDtypeStruct((1, inc), F32),
            jax.ShapeDtypeStruct((2, ells, inc, nodes), F32),
        ),
        in_specs=[hbm] * 16,
        out_specs=(vmem, vmem, vmem),
        scratch_shapes=[pltpu.SMEM(x.shape, x.dtype) for x in small]
        + [pltpu.VMEM(x.shape, x.dtype) for x in large]
        + [
            pltpu.VMEM(leaf_ops.shape, F32),
            pltpu.VMEM((ns, leaf_width, half), F32),
            pltpu.VMEM(up_ops.shape, F32),
            pltpu.VMEM((ns, leaf_width, half), BF16),
            pltpu.VMEM((vectors, ells, rows, nodes), F32),
            pltpu.VMEM((3 * ells, rows + 8, nodes), F32),
            pltpu.VMEM((ells, 8, nodes), F32),
            pltpu.VMEM((ells, nodes, 8), F32),
            pltpu.VMEM((ells, leaf_width, nodes), BF16),
            pltpu.VMEM((ells, leaf_width, nodes), BF16),
            pltpu.VMEM((3 * boxes, rows + 8, leaf_width), F32),
            pltpu.VMEM((nb, rows, half), F32),
            pltpu.VMEM((ns, rows, half), F32),
            pltpu.VMEM((nodes, nodes), BF16),
            pltpu.VMEM((nodes, nodes), BF16),
            pltpu.VMEM((ells, rows, nodes), F32),
            pltpu.VMEM((ells, rows, nodes), F32),
            pltpu.VMEM((nd, 1, 128), F32),
            dma((ns + 15,)),
            dma((2,)),
            dma((2,)),
            dma((2,)),
            dma((2,)),
            dma((nb, 3)),
            dma((nb,)),
            dma((1,)),
            dma((1,)),
            dma((nd,)),
            dma((nd,)),
        ],
        compiler_params=pltpu.CompilerParams(
            collective_id=0, has_side_effects=True, vmem_limit_bytes=67043328
        ),
    )(*small, *large, leaf_ops, interp, up_ops)
    h_column, h_norm, next_vector = pl.pallas_call(
        hand_on,
        out_shape=tuple(jax.ShapeDtypeStruct(x.shape, F32) for x in (h_column, h_norm, next_vector)),
        in_specs=[vmem] * 3,
        out_specs=(vmem, vmem, vmem),
    )(h_column, h_norm, next_vector)
    return h_column, h_norm.reshape(inc), jnp.transpose(next_vector, (0, 2, 1, 3))


def solution(mesh):
    placed = (
        P(None, None, None, ("group", "box", "sample"), None),
        P(None, ("group", "box", "sample"), None, None),
        P(None, ("group", "box", "sample"), None),
        P(("group", "box", "sample"), None),
        P(("group", "box", "sample")),
        P(("group", "box", "sample"), None),
        P(("group", "box", "sample"), None),
        P(("group", "box", "sample"), None),
        P(),
        P(),
        P(None, ("group", "box")),
        P("group", None),
        P("group", None),
        P(None, None, "sample"),
    )
    return jax.shard_map(
        functools.partial(body, mesh.shape["box"], mesh.shape["sample"]),
        mesh=mesh,
        in_specs=placed,
        out_specs=(P(None, None, "group"), P("group"), P(None, None, ("box", "sample"), "group")),
        check_vma=False,
    )
```

profile of v0, /device:TPU:0, one launch (start us, length us, event | category | flops | bytes accessed | tf_op | source)
XLA Modules:
  0.0 30.5 jit_solution(573250612039677087)
XLA Ops:
  0.6 28.5 %shard_map.175 = (f32[2,4,4]{2,1,0:T(4,128)}, f32[1,4]{1,0:T(1,128)}, f32[2,3,4,256]{3,2,1,0:T(4,128)}) custom-call(s32[3]{0:T(128)} %box_of_hbm.1, s32[3,4]{1,0:T(4,128)} %near_list_hbm.1, s32[2,4]{1,0:T(2,128)} %leaf_src_hbm.1, s32[2,4]{1,0:T(2,128)} %leaf_op_hbm.1, s32[8,6]{1,0:T(8,128)} %up_src_hbm.1, s32[8,6]{1,0:T(8,128)} %up_op_hbm.1, ...), custom_call_target="tpu_custom_call" | custom-call | tf_op jit(solution)/shard_map/pallas_call | solution.py:568
  29.2 1.4 %shard_map.176 = (f32[2,4,4]{2,1,0:T(4,128)}, f32[1,4]{1,0:T(1,128)}, f32[2,3,4,256]{3,2,1,0:T(4,128)}) custom-call(f32[2,4,4]{2,1,0:T(4,128)} %get-tuple-element.9.h_in, f32[1,4]{1,0:T(1,128)} %get-tuple-element.10.norm_in, f32[2,3,4,256]{3,2,1,0:T(4,128)} %get-tuple-element.11.next_in), custom_call_target="tpu_custom_call" | custom-call | tf_op jit(solution)/shard_map/pallas_call | solution.py:614
where the time goes:
time: 30.8 us; the launch traced here: 30.5 us
  Pallas kernels  29.9 us (97%)
  between operations  0.64 us (2%)
    pallas_call x1, Pallas kernels, body(): pl.pallas_call(functools.partial(kernel, nb, ns), out_shape=(jax.ShapeDty...  28.5 us
    pallas_call x1, Pallas kernels, body(): pl.pallas_call(hand_on, out_shape=tuple((jax.ShapeDtypeStruct(x.shape, F3...  1.37 us

commit v1 on v0

--- a/solution.py
+++ b/solution.py
@@ -13,6 +13,8 @@
 F32 = jnp.float32
 BF16 = jnp.bfloat16
 ROWS = 64
+SPAN = 128
+SPLITS = ((0, 0), (1, 0), (2, 0), (0, 1), (1, 1), (0, 2))
 
 
 def sphere_points(total):
@@ -24,21 +26,35 @@
     return np.stack(points).astype(np.float32)
 
 
-SIN_COEFS = (6.283185280261419, -10.335420167015924, 5.100155046431118, -1.1965825712511455, 0.15531532062982073)
-COS_COEFS = (0.9999999532476092, -4.9347928306196795, 4.058411352863147, -1.3318765680841478, 0.21968961110420304)
-
-
-def turn(t):
-    f = t - jnp.floor(t + 0.5)
+SIN_TABLE = (4.44286798223381, -7.307445412162602, 3.594802094687321, -0.7844036018968589)
+COS_TABLE = (1.414204080580398, -6.977642059296966, 5.715238406047747, -1.7283486673722932)
+SIN_FULL = (4.442882834891658, -7.308241184631927, 3.6062893308970487, -0.8457654001243101, 0.10920874958601288)
+COS_FULL = (1.4142134965660362, -6.978850988281385, 5.739461171112273, -1.88356298861798, 0.31069819238699753)
+
+
+def series(coefs, u):
+    total = coefs[-1]
+    for coef in coefs[-2::-1]:
+        total = total * u + coef
+    return total
+
+
+def half_turn(t, sin_coefs, cos_coefs):
+    f = t - jnp.round(t)
     u = f * f
-    s = SIN_COEFS[-1]
-    for coef in SIN_COEFS[-2::-1]:
-        s = s * u + coef
-    s = s * f
-    c = COS_COEFS[-1]
-    for coef in COS_COEFS[-2::-1]:
-        c = c * u + coef
-    return 1.0 - 0.5 * s * s, s * c
+    return series(sin_coefs, u) * f, series(cos_coefs, u)
+
+
+def turn(t, sin_coefs=SIN_TABLE, cos_coefs=COS_TABLE):
+    s, c = half_turn(t, sin_coefs, cos_coefs)
+    return 1.0 - s * s, s * c
+
+
+def thirds(x):
+    high = x.astype(BF16).astype(F32)
+    rest = x - high
+    middle = rest.astype(BF16).astype(F32)
+    return high, middle, rest - middle
 
 
 def pair(x):
@@ -95,11 +111,14 @@
     interp,
     ks,
     halo,
-    shifted,
+    phases,
     columns,
+    split_pos,
     cos_tab,
     sin_tab,
     pat,
+    give,
+    take,
     gathered,
     full,
     near_r,
@@ -118,6 +137,8 @@
     recv_d,
     send_e,
     recv_e,
+    send_f,
+    recv_f,
 ):
     nb, ns = box_count_axis, sample_count_axis
     nd = nb * ns
@@ -127,6 +148,7 @@
     near_count = near_list.shape[1]
     leaf_width = interp.shape[1]
     half = interp.shape[2]
+    pairs_total = ells * near_count
     bi = lax.axis_index("box")
     si = lax.axis_index("sample")
     dev = bi * ns + si
@@ -241,24 +263,9 @@
         for b in range(1, boxes):
             middle = middle + centers[b] * member[b][e]
         here = halo[ells + e, rows : rows + 8, :]
-        shifted[e] = here - middle
+        pieces = thirds(here - middle)
+        split_pos[e] = jnp.concatenate([pieces[p] for _, p in SPLITS], axis=0).astype(BF16)
         columns[e] = jnp.transpose(here)
-
-    def fill(chunk, carry):
-        at = pl.multiple_of(chunk * ROWS, ROWS)
-        ways = [
-            jnp.broadcast_to(leaf_dirs[pl.ds(at, ROWS), axis : axis + 1], (ROWS, nodes)) for axis in range(3)
-        ]
-        for e in range(ells):
-            t = ways[0] * shifted[e, 0:1, :]
-            for axis in range(1, 3):
-                t = t + ways[axis] * shifted[e, axis : axis + 1, :]
-            cosine, sine = turn(t)
-            cos_tab[e, pl.ds(at, ROWS), :] = cosine.astype(BF16)
-            sin_tab[e, pl.ds(at, ROWS), :] = sine.astype(BF16)
-        return carry
-
-    lax.fori_loop(0, leaf_width // ROWS, fill, 0)
 
     ready("krylov", "node_wts", "self_inv")
     for e in range(ells):
@@ -266,35 +273,16 @@
             for q in range(2):
                 ks[m, e, q * inc : (q + 1) * inc, :] = krylov[q, m, e]
     nt = (((1,), (1,)), ((), ()))
+    halves_of_values = []
     for e in range(ells):
         rounded = ks[vectors - 1, e].astype(BF16)
         c = lax.dot_general(rounded, self_inv[0, e], nt, preferred_element_type=F32)
         d = lax.dot_general(rounded, self_inv[1, e], nt, preferred_element_type=F32)
-        halo[ells + e, 0:rows, :] = inward(c, d) * node_wts[e : e + 1, :]
-
-    radiated = []
-    for e in range(ells):
-        values = halo[ells + e, 0:rows, :]
-        radiated.append(outward(both(values, cos_tab[e], 1), both(values, sin_tab[e], 1)))
-    for b in range(boxes):
-        total = radiated[0] * member[b][0]
-        for e in range(1, ells):
-            total = total + radiated[e] * member[b][e]
-        pat[boxes + b, 0:rows, :] = total
-        pat[boxes + b, rows:, :] = jnp.broadcast_to(centers[b], (8, leaf_width))
-    pl.semaphore_wait(barrier, nd - 1)
-    start_b()
-    start_a()
-
-    for h in range(ns):
-        ready(("interp", h))
-
-        def cast(chunk, carry, h=h):
-            at = pl.multiple_of(chunk * 16, 16)
-            interp[h, pl.ds(at, 16), :] = interp_raw[h, pl.ds(at, 16), :].astype(BF16)
-            return carry
-
-        lax.fori_loop(0, leaf_width // 16, cast, 0)
+        source = inward(c, d) * node_wts[e : e + 1, :]
+        halo[ells + e, 0:rows, :] = source
+        halves_of_values.append(pair(source))
+
+    ready("parent_centers", "up_dirs")
 
     def up_phase(center, dirs):
         t = (center[0:1] - parent_centers[0, 0]) * dirs[0:1]
@@ -303,81 +291,83 @@
         return t
 
     def turns_of(list_of_centers, dirs):
-        return turn(jnp.concatenate([up_phase(center, dirs) for center in list_of_centers], axis=0))
-
-    ready("parent_centers", "up_dirs")
-    arrive_b()
-    first = (1 - si) * boxes
-    children = ns * boxes
-    child_centers = [pat[first + c, rows:, 0:1] for c in range(children)]
-    child_cos, child_sin = turns_of(child_centers, up_dirs[si])
-    lifted = both(
-        jnp.concatenate([pat[first + c, 0:rows, :] for c in range(children)], axis=0), interp[si], 0
+        t = jnp.concatenate([up_phase(center, dirs) for center in list_of_centers], axis=0)
+        return turn(t, SIN_FULL, COS_FULL)
+
+    halves = (si, (si + 1) % ns)
+    for slot, h in enumerate(halves):
+        cosine, sine = turns_of(centers, up_dirs[h])
+        phases[slot, 0] = cosine
+        phases[slot, 1] = sine
+
+    for start in range(0, leaf_width, SPAN):
+        span = pl.ds(start, SPAN)
+        totals = [None] * boxes
+        for e in range(ells):
+            t = jnp.dot(leaf_dirs[span, :], split_pos[e], preferred_element_type=F32)
+            cosine, sine = turn(t)
+            cosine, sine = cosine.astype(BF16), sine.astype(BF16)
+            cos_tab[e, span, :] = cosine
+            sin_tab[e, span, :] = sine
+            c = lax.dot_general(halves_of_values[e], cosine, nt, preferred_element_type=F32)
+            d = lax.dot_general(halves_of_values[e], sine, nt, preferred_element_type=F32)
+            piece = outward(c[:rows] + c[rows:], d[:rows] + d[rows:])
+            for b in range(boxes):
+                part = piece * member[b][e]
+                totals[b] = part if e == 0 else totals[b] + part
+        for b in range(boxes):
+            pat[boxes + b, :, span] = totals[b]
+
+    for h in range(ns):
+        ready(("interp", h))
+    whole = pair(jnp.concatenate([pat[boxes + b] for b in range(boxes)], axis=0))
+
+    def lift(slot):
+        table = interp_raw[halves[slot]].astype(BF16)
+        interp[halves[slot]] = table
+        lifted = jnp.dot(whole, table, preferred_element_type=F32)
+        lifted = lifted[: boxes * rows] + lifted[boxes * rows :]
+        parent = None
+        for b in range(boxes):
+            piece = lifted[b * rows : (b + 1) * rows]
+            term = outward(
+                piece * phases[slot, 0, b : b + 1, :], piece * phases[slot, 1, b : b + 1, :]
+            )
+            parent = term if parent is None else parent + term
+        return parent
+
+    give[...] = lift(1)
+    partner_id = {"box": bi, "sample": (si + 1) % ns}
+    swap_parts = pltpu.make_async_remote_copy(
+        src_ref=give, dst_ref=take, send_sem=send_f.at[0], recv_sem=recv_f.at[0],
+        device_id=partner_id, device_id_type=MESH,
     )
-    parent = None
-    for c in range(children):
-        piece = lifted[c * rows : (c + 1) * rows]
-        term = outward(piece * child_cos[c : c + 1], piece * child_sin[c : c + 1])
-        parent = term if parent is None else parent + term
-    gathered[bi] = parent
-
-    twins = 2 if nb % 2 == 0 else 1
-    levels = nb // twins
-    level = bi // twins
-    twin = level * twins + (bi + 1) % twins
-
-    def hop(slot, way):
-        target = (twin, (bi + twins) % nb, (bi + nb - twins) % nb)[way]
+    pl.semaphore_wait(barrier, nd - 1)
+    swap_parts.start()
+    start_b()
+    start_a()
+    own_part = lift(0)
+    swap_parts.wait_recv()
+    gathered[bi] = own_part + take[...]
+
+    def deliver(off, slot):
         return pltpu.make_async_remote_copy(
-            src_ref=gathered.at[slot], dst_ref=gathered.at[slot], send_sem=send_c.at[slot, way],
-            recv_sem=recv_c.at[slot], device_id={"box": target, "sample": si}, device_id_type=MESH,
+            src_ref=gathered.at[slot], dst_ref=gathered.at[slot], send_sem=send_c.at[off],
+            recv_sem=recv_c.at[slot], device_id={"box": (bi + off) % nb, "sample": si}, device_id_type=MESH,
         )
 
-    def hand_over(slot, ways, act):
-        if twins > 1:
-            act(hop(slot, 0))
-        for way in ways:
-            room = level < levels - 1 if way == 1 else level > 0
-
-            @pl.when(room)
-            def _(way=way):
-                act(hop(slot, way))
-
-    def relay(distance, act, wait):
-        for way, there, slot in (
-            (1, level >= distance, bi - distance * twins),
-            (2, level < levels - distance, bi + distance * twins),
-        ):
-            @pl.when(there)
-            def _(way=way, slot=slot):
-                if wait:
-                    hop(slot, way).wait_recv()
-                hand_over(slot, (way,), act)
-
-    hand_over(bi, (1, 2), lambda copy: copy.start())
+    for off in range(1, nb):
+        deliver(off, bi).start()
 
     def translate(operators, index, values):
         pair_rows = operators[index]
         return inward(values * pair_rows[0:1], values * pair_rows[1:2])
 
-    ready("leaf_src", "leaf_op", "leaf_ops")
-    incoming = []
-    for b in range(boxes):
-        total = None
-        for j in range(leaf_src.shape[1]):
-            source = pat[jnp.clip(leaf_src[b, j] - (dev - 1) * boxes, 0, 3 * boxes - 1)]
-            term = translate(leaf_ops, leaf_op[b, j], source[0:rows])
-            total = term if total is None else total + term
-        incoming.append(total)
-
-    halves = (si, (si + 1) % ns)
-    own_phase = [turns_of(centers, up_dirs[h]) for h in halves]
-
     ready("near_list")
     arrive_a()
     near_acc[...] = jnp.zeros(near_acc.shape, F32)
 
-    def near_pair(index, carry):
+    def near_pair(index, slot):
         e = index // near_count
         j = index % near_count
         source = halo[jnp.clip(near_list[e, j] - (dev - 1) * ells, 0, 3 * ells - 1)]
@@ -388,30 +378,37 @@
                 gap = target[:, axis : axis + 1] - source[rows + axis : rows + axis + 1]
                 squared = gap * gap if squared is None else squared + gap * gap
             inverse = lax.rsqrt(squared)
-            cosine, sine = turn(squared * inverse)
-            near_r[chunk * ROWS : (chunk + 1) * ROWS, :] = (cosine * inverse).astype(BF16)
-            near_i[chunk * ROWS : (chunk + 1) * ROWS, :] = (sine * inverse).astype(BF16)
+            s, c = half_turn(squared * inverse, SIN_TABLE, COS_TABLE)
+            scaled = s * inverse
+            near_r[slot, chunk * ROWS : (chunk + 1) * ROWS, :] = (inverse - s * scaled).astype(BF16)
+            near_i[slot, chunk * ROWS : (chunk + 1) * ROWS, :] = (scaled * c).astype(BF16)
         values = source[0:rows]
-        near_acc[e] += inward(both(values, near_r[...], 1), both(values, near_i[...], 1))
+        near_acc[e] += inward(both(values, near_r[slot], 1), both(values, near_i[slot], 1))
+
+    group = 2 if pairs_total % 2 == 0 else 1
+
+    def near_group(index, carry):
+        for slot in range(group):
+            near_pair(index * group + slot, slot)
         return carry
 
-    pairs_total = ells * near_count
-    last = pairs_total - near_count // 2
-    share = max(1, last // (levels + 1))
-    done = 0
-    for distance in range(1, levels):
-        upto = min(done + share, last)
-        if upto > done:
-            lax.fori_loop(done, upto, near_pair, 0)
-        done = upto
-        relay(distance, lambda copy: copy.start(), True)
-    if last > done:
-        lax.fori_loop(done, last, near_pair, 0)
-    done = last
+    lax.fori_loop(0, pairs_total // group, near_group, 0)
+
+    arrive_b()
+    ready("leaf_src", "leaf_op", "leaf_ops")
+    incoming = []
+    for b in range(boxes):
+        total = None
+        for j in range(leaf_src.shape[1]):
+            source = pat[jnp.clip(leaf_src[b, j] - (dev - 1) * boxes, 0, 3 * boxes - 1)]
+            term = translate(leaf_ops, leaf_op[b, j], source)
+            total = term if total is None else total + term
+        incoming.append(total)
+
+
     ready("up_src", "up_op", "up_ops")
-    if twins > 1:
-        for other in range(levels):
-            hop(other * twins + (bi + 1) % twins, 0).wait_recv()
+    for off in range(1, nb):
+        deliver(off, (bi + off) % nb).wait_recv()
     parent_in = None
     for j in range(up_src.shape[1]):
         term = translate(up_ops, up_op[bi, j], gathered[up_src[bi, j]])
@@ -419,26 +416,25 @@
     full[si] = parent_in
     partner = pltpu.make_async_remote_copy(
         src_ref=full.at[si], dst_ref=full.at[si], send_sem=send_d.at[0], recv_sem=recv_d.at[0],
-        device_id={"box": bi, "sample": (si + 1) % ns}, device_id_type=MESH,
+        device_id=partner_id, device_id_type=MESH,
     )
     partner.start()
 
-    lax.fori_loop(done, pairs_total, near_pair, 0)
-    def lower(h, phase):
-        own_cos, own_sin = phase
+    def lower(slot):
+        h = halves[slot]
         values = full[h]
         lowered = jnp.concatenate(
             [
-                inward(values * own_cos[b : b + 1], values * own_sin[b : b + 1])
+                inward(values * phases[slot, 0, b : b + 1, :], values * phases[slot, 1, b : b + 1, :])
                 for b in range(boxes)
             ],
             axis=0,
         )
         return both(lowered, interp[h], 1)
 
-    lowered = lower(si, own_phase[0])
+    lowered = lower(0)
     partner.wait_recv()
-    lowered = lowered + lower(halves[1], own_phase[1])
+    lowered = lowered + lower(1)
     for b in range(boxes):
         incoming[b] = incoming[b] + lowered[b * rows : (b + 1) * rows]
 
@@ -515,9 +511,9 @@
     finish_a()
     finish_b()
     partner.wait_send()
-    hand_over(bi, (1, 2), lambda copy: copy.wait_send())
-    for distance in range(1, levels):
-        relay(distance, lambda copy: copy.wait_send(), False)
+    swap_parts.wait_send()
+    for off in range(1, nb):
+        deliver(off, bi).wait_send()
     for off in range(1, nd):
         pltpu.make_async_remote_copy(
             src_ref=sums.at[dev], dst_ref=sums.at[dev], send_sem=send_e.at[off], recv_sem=recv_e.at[dev],
@@ -555,8 +551,14 @@
     leaf_width, up_width = interp.shape
     half = up_ops.shape[2]
     nd = nb * ns
-    leaf_dirs = np.zeros((leaf_width, 8), np.float32)
-    leaf_dirs[:, :3] = sphere_points(leaf_width).T
+    directions = sphere_points(leaf_width).T
+    pieces = []
+    for _ in range(3):
+        pieces.append(directions.astype(BF16))
+        directions = directions - pieces[-1].astype(np.float32)
+    leaf_dirs = np.zeros((leaf_width, 8 * len(SPLITS)), BF16)
+    for block, (piece, _) in enumerate(SPLITS):
+        leaf_dirs[:, 8 * block : 8 * block + 3] = pieces[piece]
     up_dirs = np.zeros((ns, 8, half), np.float32)
     up_dirs[:, :3] = np.moveaxis(sphere_points(up_width).reshape(3, ns, half), 1, 0)
     small = [box_of, near_list, leaf_src, leaf_op, up_src, up_op, parent_centers.T]
@@ -583,15 +585,18 @@
             pltpu.VMEM((ns, leaf_width, half), BF16),
             pltpu.VMEM((vectors, ells, rows, nodes), F32),
             pltpu.VMEM((3 * ells, rows + 8, nodes), F32),
-            pltpu.VMEM((ells, 8, nodes), F32),
+            pltpu.VMEM((ns, 2, boxes, half), F32),
             pltpu.VMEM((ells, nodes, 8), F32),
+            pltpu.VMEM((ells, 8 * len(SPLITS), nodes), BF16),
             pltpu.VMEM((ells, leaf_width, nodes), BF16),
             pltpu.VMEM((ells, leaf_width, nodes), BF16),
-            pltpu.VMEM((3 * boxes, rows + 8, leaf_width), F32),
+            pltpu.VMEM((3 * boxes, rows, leaf_width), F32),
+            pltpu.VMEM((rows, half), F32),
+            pltpu.VMEM((rows, half), F32),
             pltpu.VMEM((nb, rows, half), F32),
             pltpu.VMEM((ns, rows, half), F32),
-            pltpu.VMEM((nodes, nodes), BF16),
-            pltpu.VMEM((nodes, nodes), BF16),
+            pltpu.VMEM((2, nodes, nodes), BF16),
+            pltpu.VMEM((2, nodes, nodes), BF16),
             pltpu.VMEM((ells, rows, nodes), F32),
             pltpu.VMEM((ells, rows, nodes), F32),
             pltpu.VMEM((nd, 1, 128), F32),
@@ -600,12 +605,14 @@
             dma((2,)),
             dma((2,)),
             dma((2,)),
-            dma((nb, 3)),
+            dma((nb,)),
             dma((nb,)),
             dma((1,)),
             dma((1,)),
             dma((nd,)),
             dma((nd,)),
+            dma((1,)),
+            dma((1,)),
         ],
         compiler_params=pltpu.CompilerParams(
             collective_id=0, has_side_effects=True, vmem_limit_bytes=67043328

time: 30.8 us -> 26 us (0.84)
  Pallas kernels: 29.9 us -> 25.1 us
    pallas_call x1, Pallas kernels: 28.5 us -> 23.7 us  [body(): pl.pallas_call(functools.partial(kernel, nb, ns), out_shape=(jax.ShapeDty...]
where the time goes in v1:
time: 26 us; the launch traced here: 25.8 us
  Pallas kernels  25.1 us (97%)
  between operations  0.64 us (2%)
    pallas_call x1, Pallas kernels, body(): pl.pallas_call(functools.partial(kernel, nb, ns), out_shape=(jax.ShapeDty...  23.7 us
    pallas_call x1, Pallas kernels, body(): pl.pallas_call(hand_on, out_shape=tuple((jax.ShapeDtypeStruct(x.shape, F3...  1.37 us

profile of v1, /device:TPU:0, one launch (start us, length us, event | category | flops | bytes accessed | tf_op | source)
XLA Modules:
  0.0 25.8 jit_solution(17435042114324098642)
XLA Ops:
  0.6 23.7 %shard_map.175 = (f32[2,4,4]{2,1,0:T(4,128)}, f32[1,4]{1,0:T(1,128)}, f32[2,3,4,256]{3,2,1,0:T(4,128)}) custom-call(s32[3]{0:T(128)} %box_of_hbm.1, s32[3,4]{1,0:T(4,128)} %near_list_hbm.1, s32[2,4]{1,0:T(2,128)} %leaf_src_hbm.1, s32[2,4]{1,0:T(2,128)} %leaf_op_hbm.1, s32[8,6]{1,0:T(8,128)} %up_src_hbm.1, s32[8,6]{1,0:T(8,128)} %up_op_hbm.1, ...), custom_call_target="tpu_custom_call" | custom-call | tf_op jit(solution)/shard_map/pallas_call | solution.py:570
  24.4 1.4 %shard_map.176 = (f32[2,4,4]{2,1,0:T(4,128)}, f32[1,4]{1,0:T(1,128)}, f32[2,3,4,256]{3,2,1,0:T(4,128)}) custom-call(f32[2,4,4]{2,1,0:T(4,128)} %get-tuple-element.9.h_in, f32[1,4]{1,0:T(1,128)} %get-tuple-element.10.norm_in, f32[2,3,4,256]{3,2,1,0:T(4,128)} %get-tuple-element.11.next_in), custom_call_target="tpu_custom_call" | custom-call | tf_op jit(solution)/shard_map/pallas_call | solution.py:621

commit v2 on v1

v2 whole, which is shorter than its diff:
```python
import functools
import math

import jax
import jax.numpy as jnp
import numpy as np
from jax import lax
from jax.experimental import pallas as pl
from jax.experimental.pallas import tpu as pltpu
from jax.sharding import PartitionSpec as P

MESH = pl.DeviceIdType.MESH
F32 = jnp.float32
BF16 = jnp.bfloat16
ROWS = 64
SPAN = 128
SPLITS = ((0, 0), (1, 0), (2, 0), (0, 1), (1, 1), (0, 2))


def sphere_points(total):
    position = np.arange(total).astype(np.float32)
    height = np.float32(1.0) - (np.float32(2.0) * position + np.float32(1.0)) / np.float32(total)
    radius = np.sqrt(np.float32(1.0) - height * height)
    angle = (position * np.float32(math.pi * (3.0 - math.sqrt(5.0)))).astype(np.float64)
    points = [radius * np.cos(angle).astype(np.float32), radius * np.sin(angle).astype(np.float32), height]
    return np.stack(points).astype(np.float32)


SIN_TABLE = (4.44286798223381, -7.307445412162602, 3.594802094687321, -0.7844036018968589)
COS_TABLE = (1.414204080580398, -6.977642059296966, 5.715238406047747, -1.7283486673722932)
SIN_FULL = (4.442882834891658, -7.308241184631927, 3.6062893308970487, -0.8457654001243101, 0.10920874958601288)
COS_FULL = (1.4142134965660362, -6.978850988281385, 5.739461171112273, -1.88356298861798, 0.31069819238699753)


def series(coefs, u):
    total = coefs[-1]
    for coef in coefs[-2::-1]:
        total = total * u + coef
    return total


def half_turn(t, sin_coefs, cos_coefs):
    f = t - jnp.round(t)
    u = f * f
    return series(sin_coefs, u) * f, series(cos_coefs, u)


def turn(t, sin_coefs=SIN_TABLE, cos_coefs=COS_TABLE):
    s, c = half_turn(t, sin_coefs, cos_coefs)
    return 1.0 - s * s, s * c


def thirds(x):
    high = x.astype(BF16).astype(F32)
    rest = x - high
    middle = rest.astype(BF16).astype(F32)
    return high, middle, rest - middle


def pair(x):
    high = x.astype(BF16).astype(F32)
    return jnp.concatenate([high, x - high], axis=0).astype(BF16)


def both(x, table, contract):
    rows = x.shape[0]
    out = lax.dot_general(
        pair(x), table, (((1,), (contract,)), ((), ())), preferred_element_type=F32
    )
    return out[:rows] + out[rows:]


def kernel(
    box_count_axis,
    sample_count_axis,
    box_of_hbm,
    near_list_hbm,
    leaf_src_hbm,
    leaf_op_hbm,
    up_src_hbm,
    up_op_hbm,
    parent_centers_hbm,
    krylov_hbm,
    self_inv_hbm,
    node_pos_hbm,
    node_wts_hbm,
    leaf_dirs_hbm,
    up_dirs_hbm,
    leaf_ops_hbm,
    interp_hbm,
    up_ops_hbm,
    small_hbm,
    next_hbm,
    box_of,
    near_list,
    leaf_src,
    leaf_op,
    up_src,
    up_op,
    parent_centers,
    krylov,
    self_inv,
    node_pos,
    node_wts,
    leaf_dirs,
    up_dirs,
    leaf_ops,
    interp_raw,
    up_ops,
    interp,
    ks,
    halo,
    phases,
    columns,
    split_pos,
    turns,
    cos_tab,
    sin_tab,
    pat,
    give,
    take,
    parents,
    gathered,
    cross,
    full,
    squares,
    near_r,
    near_i,
    near_acc,
    result,
    sums,
    local_sem,
    recv_a,
    recv_b,
    recv_sem,
    small_out,
    next_out,
):
    nb, ns = box_count_axis, sample_count_axis
    nd = nb * ns
    _, vectors, ells, inc, nodes = krylov.shape
    rows = 2 * inc
    boxes = leaf_src.shape[0]
    near_count = near_list.shape[1]
    twins, leaf_width, part = interp.shape[1:]
    half = twins * part
    pairs_total = ells * near_count
    bi = lax.axis_index("box")
    si = lax.axis_index("sample")
    dev = bi * ns + si
    levels = nb // twins
    level = bi // twins
    twin = bi % twins

    def load(slot, source, target):
        copy = pltpu.make_async_copy(source, target, local_sem.at[slot])
        copy.start()
        return copy

    loads = {}

    def begin(**arrays):
        for name, (source, target) in arrays.items():
            loads[name] = load(len(loads), source, target)

    def ready(*wanted):
        for name in wanted:
            loads[name].wait()

    def place(index):
        return {"box": index // ns, "sample": index % ns}

    begin(node_pos=(node_pos_hbm, node_pos), box_of=(box_of_hbm, box_of), leaf_dirs=(leaf_dirs_hbm, leaf_dirs))
    barrier = pltpu.get_barrier_semaphore()
    for off in range(1, nd):
        pl.semaphore_signal(barrier, inc=1, device_id=place((dev + off) % nd), device_id_type=MESH)
    begin(
        krylov=(krylov_hbm, krylov), node_wts=(node_wts_hbm, node_wts), self_inv=(self_inv_hbm, self_inv),
        parent_centers=(parent_centers_hbm, parent_centers), up_dirs=(up_dirs_hbm, up_dirs),
    )
    halves = (si, (si + 1) % ns)
    for slot in range(ns - 1, -1, -1):
        at = pl.ds(pl.multiple_of(halves[slot] * half, half), half)
        loads["interp", slot] = load(len(loads), interp_hbm.at[:, at], interp_raw.at[slot])
    begin(
        near_list=(near_list_hbm, near_list), leaf_src=(leaf_src_hbm, leaf_src), leaf_op=(leaf_op_hbm, leaf_op),
        up_src=(up_src_hbm, up_src), up_op=(up_op_hbm, up_op), up_ops=(up_ops_hbm.at[:, :, pl.ds(pl.multiple_of(twin * part, part), part)], up_ops),
        leaf_ops=(leaf_ops_hbm, leaf_ops),
    )

    sign = jnp.where(lax.broadcasted_iota(jnp.int32, (rows, 1), 0) < inc, 1.0, -1.0)

    def swap(x):
        return pltpu.roll(x, inc, 0)

    def inward(c, d):
        return c - sign * swap(d)

    def outward(c, d):
        return c + sign * swap(d)

    def neighbours(buffer, width, send, recv):
        own = buffer.at[pl.ds(width, width)]
        right = pltpu.make_async_remote_copy(
            src_ref=own, dst_ref=buffer.at[pl.ds(0, width)], send_sem=local_sem.at[send], recv_sem=recv.at[0],
            device_id=place((dev + 1) % nd), device_id_type=MESH,
        )
        left = pltpu.make_async_remote_copy(
            src_ref=own, dst_ref=buffer.at[pl.ds(2 * width, width)], send_sem=local_sem.at[send + 1], recv_sem=recv.at[1],
            device_id=place((dev + nd - 1) % nd), device_id_type=MESH,
        )

        def start():
            @pl.when(dev < nd - 1)
            def _():
                right.start()

            @pl.when(dev > 0)
            def _():
                left.start()

        def arrive():
            @pl.when(dev > 0)
            def _():
                right.wait_recv()

            @pl.when(dev < nd - 1)
            def _():
                left.wait_recv()

        def finish():
            @pl.when(dev < nd - 1)
            def _():
                right.wait_send()

            @pl.when(dev > 0)
            def _():
                left.wait_send()

        return start, arrive, finish

    start_a, arrive_a, finish_a = neighbours(halo, ells, 0, recv_a)
    start_b, arrive_b, finish_b = neighbours(pat, boxes, 2, recv_b)

    ready("node_pos", "box_of", "leaf_dirs")
    for e in range(ells):
        for axis in range(3):
            halo[ells + e, rows + axis : rows + axis + 1, :] = node_pos[axis, e : e + 1, :]
        halo[ells + e, rows + 3 :, :] = jnp.zeros((halo.shape[1] - rows - 3, nodes), F32)

    member = [
        [jnp.where(box_of[e] - dev * boxes == b, 1.0, 0.0) for e in range(ells)] for b in range(boxes)
    ]
    position_sum = [
        jnp.sum(halo[ells + e, rows : rows + 8, :], axis=1, keepdims=True) for e in range(ells)
    ]
    centers = []
    for b in range(boxes):
        total = position_sum[0] * member[b][0]
        amount = member[b][0]
        for e in range(1, ells):
            total = total + position_sum[e] * member[b][e]
            amount = amount + member[b][e]
        centers.append(total / (jnp.full((8, 1), 1.0, F32) * (amount * nodes)))
    for e in range(ells):
        middle = centers[0] * member[0][e]
        for b in range(1, boxes):
            middle = middle + centers[b] * member[b][e]
        here = halo[ells + e, rows : rows + 8, :]
        pieces = thirds(here - middle)
        split_pos[e] = jnp.concatenate([pieces[p] for _, p in SPLITS], axis=0).astype(BF16)

    nt = (((1,), (1,)), ((), ()))
    spans = [pl.ds(start, SPAN) for start in range(0, leaf_width, SPAN)]

    def angles(e, span):
        turns[e, span, :] = jnp.dot(leaf_dirs[span, :], split_pos[e], preferred_element_type=F32)

    def fill(e, span):
        cosine, sine = turn(turns[e, span, :])
        cos_tab[e, span, :] = cosine.astype(BF16)
        sin_tab[e, span, :] = sine.astype(BF16)

    def gather_up(e, span):
        c = lax.dot_general(pairs[e], cos_tab[e, span, :], nt, preferred_element_type=F32)
        d = lax.dot_general(pairs[e], sin_tab[e, span, :], nt, preferred_element_type=F32)
        piece = outward(c[:rows] + c[rows:], d[:rows] + d[rows:])
        for b in range(boxes):
            part = piece * member[b][e]
            pat[boxes + b, :, span] = part if e == 0 else pat[boxes + b, :, span] + part

    for span in spans:
        angles(0, span)
    for span in spans:
        if ells > 1:
            angles(1, span)
        fill(0, span)

    ready("krylov", "node_wts", "self_inv", "parent_centers", "up_dirs")
    pairs = []
    for e in range(ells):
        rounded = jnp.concatenate([krylov[q, vectors - 1, e] for q in range(2)], axis=0).astype(BF16)
        c = lax.dot_general(rounded, self_inv[0, e], nt, preferred_element_type=F32)
        d = lax.dot_general(rounded, self_inv[1, e], nt, preferred_element_type=F32)
        source = inward(c, d) * node_wts[e : e + 1, :]
        halo[ells + e, 0:rows, :] = source
        pairs.append(pair(source))


    def up_phase(center, dirs):
        t = (center[0:1] - parent_centers[0, 0]) * dirs[0:1]
        for axis in range(1, 3):
            t = t + (center[axis : axis + 1] - parent_centers[0, axis]) * dirs[axis : axis + 1]
        return t

    def turns_of(list_of_centers, dirs):
        t = jnp.concatenate([up_phase(center, dirs) for center in list_of_centers], axis=0)
        return turn(t, SIN_FULL, COS_FULL)

    for slot, h in enumerate(halves):
        cosine, sine = turns_of(centers, up_dirs[h])
        for t in range(twins):
            phases[slot, t, 0] = cosine[:, t * part : (t + 1) * part]
            phases[slot, t, 1] = sine[:, t * part : (t + 1) * part]

    pending = [(0, span) for span in spans] if ells > 1 else []
    for e in range(min(1, ells - 1), ells):
        for span in spans:
            if e + 1 < ells:
                angles(e + 1, span)
            if e > 0:
                fill(e, span)
            for _ in range(min(len(pending), 2 if e > 1 else 1)):
                gather_up(*pending.pop(0))
            pending.append((e, span))
    for item in pending:
        gather_up(*item)

    pl.semaphore_wait(barrier, nd - 1)
    start_a()
    whole = pair(jnp.concatenate([pat[boxes + b] for b in range(boxes)], axis=0))

    def lift(slot):
        ready(("interp", slot))
        parents = []
        for t in range(twins):
            table = interp_raw[slot, :, t * part : (t + 1) * part].astype(BF16)
            interp[slot, t] = table
            lifted = jnp.dot(whole, table, preferred_element_type=F32)
            lifted = lifted[: boxes * rows] + lifted[boxes * rows :]
            parent = None
            for b in range(boxes):
                piece = lifted[b * rows : (b + 1) * rows]
                term = outward(
                    piece * phases[slot, t, 0, b : b + 1, :], piece * phases[slot, t, 1, b : b + 1, :]
                )
                parent = term if parent is None else parent + term
            parents.append(parent)
        return parents

    for t, parent in enumerate(lift(1)):
        give[t] = parent
    partner_id = {"box": bi, "sample": (si + 1) % ns}
    swap_parts = pltpu.make_async_remote_copy(
        src_ref=give, dst_ref=take, send_sem=local_sem.at[4], recv_sem=recv_sem.at[0],
        device_id=partner_id, device_id_type=MESH,
    )
    swap_parts.start()
    own_part = lift(0)
    swap_parts.wait_recv()
    for t in range(twins):
        parents[t] = own_part[t] + take[t]

    def bulk(ref, send, receive):
        return pltpu.make_async_remote_copy(
            src_ref=ref, dst_ref=ref, send_sem=local_sem.at[send], recv_sem=recv_sem.at[receive],
            device_id=partner_id, device_id_type=MESH,
        )

    def deliver(box):
        pltpu.make_async_remote_copy(
            src_ref=parents.at[box % twins], dst_ref=gathered.at[bi], send_sem=local_sem.at[5],
            recv_sem=recv_sem.at[1], device_id={"box": box, "sample": si}, device_id_type=MESH,
        ).start()

    for distance in range(levels - 1, 0, -1):
        for there, up in ((level + distance < levels, 1), (level >= distance, -1)):
            @pl.when(there)
            def _(distance=distance, up=up):
                for turned in range(twins):
                    deliver((level + up * distance) * twins + (bi + turned) % twins)
    if twins > 1:
        deliver(level * twins + (bi + 1) % twins)
    every_parent = bulk(gathered.at[pl.ds(0, nb - 1)], 5, 1)
    gathered[bi] = parents[twin]
    start_b()

    def edge(x, first, ones):
        parts = thirds(jnp.sum(x * x, axis=0, keepdims=True))
        at = lax.broadcasted_iota(jnp.int32, x.shape, 0)
        block = jnp.where((at >= ones) & (at < ones + 3), 1.0, 0.0)
        for p in range(3):
            block = jnp.where(at == first + p, jnp.broadcast_to(parts[p], x.shape), block)
        return block

    for e in range(ells):
        x = halo[ells + e, rows : rows + 8, :] - position_sum[e] * (1.0 / nodes)
        pieces = thirds(-2.0 * x)
        blocks = [pieces[p] for p, _ in SPLITS] + [edge(x, 3, 0)]
        blocks.append(jnp.zeros_like(x))
        columns[e] = jnp.transpose(jnp.concatenate(blocks, axis=0)).astype(BF16)
        for m in range(vectors):
            for q in range(2):
                ks[m, e, q * inc : (q + 1) * inc, :] = krylov[q, m, e]

    def translate(operators, index, values):
        pair_rows = operators[index]
        return inward(values * pair_rows[0:1], values * pair_rows[1:2])

    ready("near_list")
    arrive_a()
    near_acc[...] = jnp.zeros(near_acc.shape, F32)

    near_items = [(e, j) for e in range(ells) for j in range(near_count)]

    def near_source(e, j):
        return halo[jnp.clip(near_list[e, j] - (dev - 1) * ells, 0, 3 * ells - 1)]

    def distances(index):
        e, j = near_items[index]
        y = near_source(e, j)[rows : rows + 8] - position_sum[e] * (1.0 / nodes)
        pieces = thirds(y)
        blocks = [pieces[p] for _, p in SPLITS] + [edge(y, 0, 3), jnp.zeros_like(y)]
        split = jnp.concatenate(blocks, axis=0).astype(BF16)
        for chunk in range(0, nodes, ROWS):
            squares[index % 2, chunk : chunk + ROWS, :] = jnp.dot(
                columns[e, chunk : chunk + ROWS, :], split, preferred_element_type=F32
            )

    def near_pair(index):
        e, j = near_items[index]
        slot = index % 2
        for chunk in range(0, nodes, ROWS):
            squared = squares[slot, chunk : chunk + ROWS, :]
            inverse = lax.rsqrt(squared)
            s, c = half_turn(squared * inverse, SIN_TABLE, COS_TABLE)
            scaled = s * inverse
            near_r[slot, chunk : chunk + ROWS, :] = (inverse - s * scaled).astype(BF16)
            near_i[slot, chunk : chunk + ROWS, :] = (scaled * c).astype(BF16)
        values = near_source(e, j)[0:rows]
        near_acc[e] += inward(both(values, near_r[slot], 1), both(values, near_i[slot], 1))

    distances(0)
    for index in range(pairs_total):
        if index + 1 < pairs_total:
            distances(index + 1)
        near_pair(index)

    ready("up_src", "up_op", "up_ops")
    every_parent.wait_recv()

    def coarse(box):
        total = None
        for j in range(up_src.shape[1]):
            term = translate(up_ops, up_op[box, j], gathered[up_src[box, j]])
            total = term if total is None else total + term
        return total

    def hand(source, receive, box, sample):
        pltpu.make_async_remote_copy(
            src_ref=source, dst_ref=full.at[si, twin], send_sem=local_sem.at[6], recv_sem=recv_sem.at[receive],
            device_id={"box": box, "sample": sample}, device_id_type=MESH,
        ).start()

    other_twin = (twin + 1) % twins
    handed = 1
    if twins > 1:
        other_box = level * twins + other_twin
        cross[...] = coarse(other_box)
        for off in range(ns - 1, -1, -1):
            hand(cross, 3, other_box, (si + off) % ns)
        handed += ns
    full[si, twin] = coarse(bi)
    hand(full.at[si, twin], 2, bi, (si + 1) % ns)

    arrive_b()
    ready("leaf_src", "leaf_op", "leaf_ops")
    incoming = []
    for b in range(boxes):
        total = None
        for j in range(leaf_src.shape[1]):
            source = pat[jnp.clip(leaf_src[b, j] - (dev - 1) * boxes, 0, 3 * boxes - 1)]
            term = translate(leaf_ops, leaf_op[b, j], source)
            total = term if total is None else total + term
        incoming.append(total)


    def lower(slot, t):
        values = full[halves[slot], t]
        lowered = jnp.concatenate(
            [
                inward(values * phases[slot, t, 0, b : b + 1, :], values * phases[slot, t, 1, b : b + 1, :])
                for b in range(boxes)
            ],
            axis=0,
        )
        return both(lowered, interp[slot, t], 1)

    lowered = lower(0, twin)
    bulk(cross, 6, 2).wait_recv()
    lowered = lowered + lower(1, twin)
    if twins > 1:
        bulk(gathered.at[pl.ds(0, ns)], 6, 3).wait_recv()
        for slot in range(ns):
            lowered = lowered + lower(slot, other_twin)
    for b in range(boxes):
        incoming[b] = incoming[b] + lowered[b * rows : (b + 1) * rows]

    lane = lax.broadcasted_iota(jnp.int32, (rows, 128), 1)
    row = lax.broadcasted_iota(jnp.int32, (rows, 128), 0)
    square = jnp.zeros((rows, 1), F32)
    straight = [jnp.zeros((rows, 1), F32) for _ in range(vectors)]
    crossed = [jnp.zeros((rows, 1), F32) for _ in range(vectors)]
    for e in range(ells):
        arriving = incoming[0] * member[0][e]
        for b in range(1, boxes):
            arriving = arriving + incoming[b] * member[b][e]
        far = inward(both(arriving, cos_tab[e], 0), both(arriving, sin_tab[e], 0))
        value = ks[vectors - 1, e] + near_acc[e] + far * leaf_width ** (-0.5)
        result[e] = value
        other = swap(value)
        square = square + jnp.sum(value * value, axis=1, keepdims=True)
        for m in range(vectors):
            basis = ks[m, e]
            straight[m] = straight[m] + jnp.sum(basis * value, axis=1, keepdims=True)
            crossed[m] = crossed[m] + jnp.sum(basis * other, axis=1, keepdims=True)
    packed = jnp.where(lane == vectors * rows + row, jnp.broadcast_to(square, lane.shape), 0.0)
    for m in range(vectors):
        a = jnp.broadcast_to(straight[m], lane.shape)
        b = jnp.broadcast_to(crossed[m], lane.shape)
        dots = jnp.where(row < inc, a + swap(a), swap(b) - b)
        packed = packed + jnp.where(lane == m * rows + row, dots, 0.0)
    sums[dev] = jnp.sum(packed, axis=0, keepdims=True)
    def share(box, sample):
        pltpu.make_async_remote_copy(
            src_ref=sums.at[dev], dst_ref=sums.at[dev], send_sem=local_sem.at[7], recv_sem=recv_sem.at[4],
            device_id={"box": box, "sample": sample}, device_id_type=MESH,
        ).start()

    for distance in range(levels - 1, 0, -1):
        for there, up in ((level + distance < levels, 1), (level >= distance, -1)):
            @pl.when(there)
            def _(distance=distance, up=up):
                for turned in range(twins):
                    for flip in range(ns):
                        share((level + up * distance) * twins + (bi + turned) % twins, (si + flip) % ns)
    for near in range(twins * ns - 1, 0, -1):
        share(level * twins + (bi + near // ns) % twins, (si + near % ns) % ns)
    every_sum = bulk(sums.at[pl.ds(0, nd - 1)], 7, 4)
    every_sum.wait_recv()
    total = sums[0]
    for index in range(1, nd):
        total = total + sums[index]
    total = total * (1.0 / (ells * nodes * nd))
    spread = jnp.broadcast_to(total, lane.shape)

    def column(start):
        return jnp.sum(
            jnp.where(lane == start + lax.rem(row, inc), spread, 0.0), axis=1, keepdims=True
        )

    real = [column(m * rows) for m in range(vectors)]
    imag = [column(m * rows + inc) for m in range(vectors)]
    norm_sq = column(vectors * rows) + column(vectors * rows + inc)
    for m in range(vectors):
        norm_sq = norm_sq - (real[m] * real[m] + imag[m] * imag[m])
    norm = jnp.sqrt(norm_sq)
    for m in range(vectors):
        for q in range(2):
            at = m * rows + q * inc
            small_out[q * vectors + m : q * vectors + m + 1, 0:inc] = total[:, at : at + inc]
    flat = jnp.sum(
        jnp.where((lane == row) & (row < inc), jnp.broadcast_to(norm, lane.shape), 0.0), axis=0, keepdims=True
    )
    small_out[2 * vectors : 2 * vectors + 1, :] = flat
    for e in range(ells):
        kept = result[e]
        for m in range(vectors):
            basis = ks[m, e]
            kept = kept - inward(basis * real[m], basis * imag[m])
        kept = kept / norm
        for q in range(2):
            next_out[q, e] = kept[q * inc : (q + 1) * inc]
    outs = [
        pltpu.make_async_copy(next_out, next_hbm, local_sem.at[8]),
        pltpu.make_async_copy(small_out, small_hbm, local_sem.at[9]),
    ]
    for copy in outs:
        copy.start()

    finish_a()
    finish_b()
    bulk(gathered.at[pl.ds(0, handed)], 6, 2).wait_send()
    swap_parts.wait_send()
    every_parent.wait_send()
    every_sum.wait_send()
    for copy in outs:
        copy.wait()


def hand_on(small_in, next_in, h_out, norm_out, next_out):
    _, vectors, inc = h_out.shape
    next_out[...] = next_in[...]
    for q in range(2):
        h_out[q] = small_in[q * vectors : (q + 1) * vectors, 0:inc]
    norm_out[...] = small_in[2 * vectors : 2 * vectors + 1, 0:inc]


def body(
    nb,
    ns,
    krylov,
    self_inv,
    node_pos,
    node_wts,
    box_of,
    near_list,
    leaf_src,
    leaf_op,
    leaf_ops,
    interp,
    parent_centers,
    up_src,
    up_op,
    up_ops,
):
    _, vectors, inc, ells, nodes = krylov.shape
    rows = 2 * inc
    boxes = leaf_src.shape[0]
    leaf_width, up_width = interp.shape
    half = up_ops.shape[2]
    nd = nb * ns
    twins = 2 if nb % 2 == 0 else 1
    part = half // twins
    directions = sphere_points(leaf_width).T
    pieces = []
    for _ in range(3):
        pieces.append(directions.astype(BF16))
        directions = directions - pieces[-1].astype(np.float32)
    leaf_dirs = np.zeros((leaf_width, 8 * len(SPLITS)), BF16)
    for block, (piece, _) in enumerate(SPLITS):
        leaf_dirs[:, 8 * block : 8 * block + 3] = pieces[piece]
    up_dirs = np.zeros((ns, 8, half), np.float32)
    up_dirs[:, :3] = np.moveaxis(sphere_points(up_width).reshape(3, ns, half), 1, 0)
    small = [box_of, near_list, leaf_src, leaf_op, up_src, up_op, parent_centers.T]
    large = [jnp.transpose(krylov, (0, 1, 3, 2, 4)), self_inv, node_pos, node_wts]
    large += [jnp.asarray(leaf_dirs), jnp.asarray(up_dirs)]
    vmem = pl.BlockSpec(memory_space=pltpu.VMEM)
    hbm = pl.BlockSpec(memory_space=pl.ANY)
    dma = pltpu.SemaphoreType.DMA
    shapes = (
        jax.ShapeDtypeStruct((2, vectors, inc), F32),
        jax.ShapeDtypeStruct((1, inc), F32),
        jax.ShapeDtypeStruct((2, ells, inc, nodes), F32),
    )
    small_shape = jax.ShapeDtypeStruct((16 * ((2 * vectors + 16) // 16), 128), F32)
    small_rows, next_rows = pl.pallas_call(
        functools.partial(kernel, nb, ns),
        out_shape=(small_shape, shapes[2]),
        in_specs=[hbm] * 16,
        out_specs=(hbm, hbm),
        scratch_shapes=[pltpu.SMEM(x.shape, x.dtype) for x in small]
        + [pltpu.VMEM(x.shape, x.dtype) for x in large]
        + [
            pltpu.VMEM(leaf_ops.shape, F32),
            pltpu.VMEM((ns, leaf_width, half), F32),
            pltpu.VMEM((*up_ops.shape[:2], part), F32),
            pltpu.VMEM((ns, twins, leaf_width, part), BF16),
            pltpu.VMEM((vectors, ells, rows, nodes), F32),
            pltpu.VMEM((3 * ells, rows + 8, nodes), F32),
            pltpu.VMEM((ns, twins, 2, boxes, part), F32),
            pltpu.VMEM((ells, nodes, 8 * len(SPLITS) + 16), BF16),
            pltpu.VMEM((ells, 8 * len(SPLITS), nodes), BF16),
            pltpu.VMEM((ells, leaf_width, nodes), F32),
            pltpu.VMEM((ells, leaf_width, nodes), BF16),
            pltpu.VMEM((ells, leaf_width, nodes), BF16),
            pltpu.VMEM((3 * boxes, rows, leaf_width), F32),
            pltpu.VMEM((twins, rows, part), F32),
            pltpu.VMEM((twins, rows, part), F32),
            pltpu.VMEM((twins, rows, part), F32),
            pltpu.VMEM((nb, rows, part), F32),
            pltpu.VMEM((rows, part), F32),
            pltpu.VMEM((ns, twins, rows, part), F32),
            pltpu.VMEM((2, nodes, nodes), F32),
            pltpu.VMEM((2, nodes, nodes), BF16),
            pltpu.VMEM((2, nodes, nodes), BF16),
            pltpu.VMEM((ells, rows, nodes), F32),
            pltpu.VMEM((ells, rows, nodes), F32),
            pltpu.VMEM((nd, 1, 128), F32),
            dma((ns + 15,)),
            dma((2,)),
            dma((2,)),
            dma((5,)),
            pltpu.VMEM(small_shape.shape, F32),
            pltpu.VMEM(shapes[2].shape, F32),
        ],
        compiler_params=pltpu.CompilerParams(
            collective_id=0, has_side_effects=True, vmem_limit_bytes=67043328
        ),
    )(*small, *large, leaf_ops, interp, up_ops)
    h_column, h_norm, next_vector = pl.pallas_call(
        hand_on,
        out_shape=shapes,
        in_specs=[vmem] * 2,
        out_specs=(vmem, vmem, vmem),
    )(small_rows, next_rows)
    return h_column, h_norm.reshape(inc), jnp.transpose(next_vector, (0, 2, 1, 3))


def solution(mesh):
    placed = (
        P(None, None, None, ("group", "box", "sample"), None),
        P(None, ("group", "box", "sample"), None, None),
        P(None, ("group", "box", "sample"), None),
        P(("group", "box", "sample"), None),
        P(("group", "box", "sample")),
        P(("group", "box", "sample"), None),
        P(("group", "box", "sample"), None),
        P(("group", "box", "sample"), None),
        P(),
        P(),
        P(None, ("group", "box")),
        P("group", None),
        P("group", None),
        P(None, None, "sample"),
    )
    return jax.shard_map(
        functools.partial(body, mesh.shape["box"], mesh.shape["sample"]),
        mesh=mesh,
        in_specs=placed,
        out_specs=(P(None, None, "group"), P("group"), P(None, None, ("box", "sample"), "group")),
        check_vma=False,
    )
```

time: 26 us -> 23.3 us (0.90)
  Pallas kernels: 25.1 us -> 22.4 us
    pallas_call x2, Pallas kernels: 25.1 us -> 22.4 us  [the longest x1 21 us: body(): pl.pallas_call(functools.partial(kernel, nb, ns), out_shape=(small_shape,...]
where the time goes in v2:
time: 23.3 us; the launch traced here: 23 us
  Pallas kernels  22.4 us (96%)
  between operations  0.64 us (3%)
    pallas_call x1, Pallas kernels, body(): pl.pallas_call(functools.partial(kernel, nb, ns), out_shape=(small_shape,...  21 us
    pallas_call x1, Pallas kernels, body(): pl.pallas_call(hand_on, out_shape=shapes, in_specs=[vmem] * 2, out_specs=...  1.37 us

profile of v2, /device:TPU:0, one launch (start us, length us, event | category | flops | bytes accessed | tf_op | source)
XLA Modules:
  0.0 23.0 jit_solution(18012261347895568799)
XLA Ops:
  0.6 21.0 %shard_map.175 = (f32[16,128]{1,0:T(8,128)}, f32[2,3,4,256]{3,2,1,0:T(4,128)}) custom-call(s32[3]{0:T(128)} %box_of_hbm.1, s32[3,4]{1,0:T(4,128)} %near_list_hbm.1, s32[2,4]{1,0:T(2,128)} %leaf_src_hbm.1, s32[2,4]{1,0:T(2,128)} %leaf_op_hbm.1, s32[8,6]{1,0:T(8,128)} %up_src_hbm.1, s32[8,6]{1,0:T(8,128)} %up_op_hbm.1, f32[1,3]{1,0:T(1,128)} %bitcast.5, ...), custom_call_target="tpu_custom_call" | custom-call | tf_op jit(solution)/shard_map/pallas_call | solution.py:667
  21.6 1.4 %shard_map.176 = (f32[2,4,4]{2,1,0:T(4,128)}, f32[1,4]{1,0:T(1,128)}, f32[2,3,4,256]{3,2,1,0:T(4,128)}) custom-call(f32[16,128]{1,0:T(8,128)} %get-tuple-element.8.small_in, f32[2,3,4,256]{3,2,1,0:T(4,128)} %get-tuple-element.9.next_in), custom_call_target="tpu_custom_call" | custom-call | tf_op jit(solution)/shard_map/pallas_call | solution.py:711

commit v3 on v2

--- a/solution.py
+++ b/solution.py
@@ -14,6 +14,8 @@
 BF16 = jnp.bfloat16
 ROWS = 64
 SPAN = 128
+TEAM = 4
+LATE = 8
 SPLITS = ((0, 0), (1, 0), (2, 0), (0, 1), (1, 1), (0, 2))
 
 
@@ -89,8 +91,8 @@
     leaf_ops_hbm,
     interp_hbm,
     up_ops_hbm,
-    small_hbm,
-    next_hbm,
+    sums_hbm,
+    result_hbm,
     box_of,
     near_list,
     leaf_src,
@@ -128,13 +130,11 @@
     near_i,
     near_acc,
     result,
-    sums,
+    share_row,
     local_sem,
     recv_a,
     recv_b,
     recv_sem,
-    small_out,
-    next_out,
 ):
     nb, ns = box_count_axis, sample_count_axis
     nd = nb * ns
@@ -142,15 +142,24 @@
     rows = 2 * inc
     boxes = leaf_src.shape[0]
     near_count = near_list.shape[1]
-    twins, leaf_width, part = interp.shape[1:]
-    half = twins * part
+    team, leaf_width, part = interp.shape[1:]
+    half = team * part
     pairs_total = ells * near_count
     bi = lax.axis_index("box")
     si = lax.axis_index("sample")
     dev = bi * ns + si
+    twins = 2 if nb % 2 == 0 else 1
     levels = nb // twins
     level = bi // twins
-    twin = bi % twins
+    member_of_team = bi % team
+    groups = nb // team
+
+    def wrapped(value, size):
+        return jnp.where(value >= size, value - size, value)
+
+    own_group = bi // team
+    bases = [wrapped(own_group + 1 + g, groups) * team for g in range(groups - 1)] + [own_group * team]
+    cores = [si] + [wrapped(si + flip, ns) for flip in range(1, ns)]
 
     def load(slot, source, target):
         copy = pltpu.make_async_copy(source, target, local_sem.at[slot])
@@ -170,23 +179,33 @@
     def place(index):
         return {"box": index // ns, "sample": index % ns}
 
-    begin(node_pos=(node_pos_hbm, node_pos), box_of=(box_of_hbm, box_of), leaf_dirs=(leaf_dirs_hbm, leaf_dirs))
+    begin(box_of=(box_of_hbm, box_of), node_pos=(node_pos_hbm, node_pos), leaf_dirs=(leaf_dirs_hbm, leaf_dirs))
     barrier = pltpu.get_barrier_semaphore()
-    for off in range(1, nd):
-        pl.semaphore_signal(barrier, inc=1, device_id=place((dev + off) % nd), device_id_type=MESH)
+    def all_others(act):
+        for base in bases[:-1]:
+            for t in range(team):
+                for core in cores:
+                    act(base + t, core)
+        for turn_by in range(team):
+            for core in cores[1 if turn_by == 0 else 0 :]:
+                act(bases[-1] + wrapped(member_of_team + turn_by, team), core)
+
+    all_others(
+        lambda box, core: pl.semaphore_signal(
+            barrier, inc=1, device_id={"box": box, "sample": core}, device_id_type=MESH
+        )
+    )
     begin(
         krylov=(krylov_hbm, krylov), node_wts=(node_wts_hbm, node_wts), self_inv=(self_inv_hbm, self_inv),
         parent_centers=(parent_centers_hbm, parent_centers), up_dirs=(up_dirs_hbm, up_dirs),
     )
-    halves = (si, (si + 1) % ns)
-    for slot in range(ns - 1, -1, -1):
+    halves = cores[:2]
+
+    def begin_interp(slot):
         at = pl.ds(pl.multiple_of(halves[slot] * half, half), half)
         loads["interp", slot] = load(len(loads), interp_hbm.at[:, at], interp_raw.at[slot])
-    begin(
-        near_list=(near_list_hbm, near_list), leaf_src=(leaf_src_hbm, leaf_src), leaf_op=(leaf_op_hbm, leaf_op),
-        up_src=(up_src_hbm, up_src), up_op=(up_op_hbm, up_op), up_ops=(up_ops_hbm.at[:, :, pl.ds(pl.multiple_of(twin * part, part), part)], up_ops),
-        leaf_ops=(leaf_ops_hbm, leaf_ops),
-    )
+
+    begin_interp(1)
 
     sign = jnp.where(lax.broadcasted_iota(jnp.int32, (rows, 1), 0) < inc, 1.0, -1.0)
 
@@ -242,7 +261,7 @@
     start_a, arrive_a, finish_a = neighbours(halo, ells, 0, recv_a)
     start_b, arrive_b, finish_b = neighbours(pat, boxes, 2, recv_b)
 
-    ready("node_pos", "box_of", "leaf_dirs")
+    ready("node_pos", "box_of")
     for e in range(ells):
         for axis in range(3):
             halo[ells + e, rows + axis : rows + axis + 1, :] = node_pos[axis, e : e + 1, :]
@@ -289,6 +308,7 @@
             part = piece * member[b][e]
             pat[boxes + b, :, span] = part if e == 0 else pat[boxes + b, :, span] + part
 
+    ready("leaf_dirs")
     for span in spans:
         angles(0, span)
     for span in spans:
@@ -297,6 +317,13 @@
         fill(0, span)
 
     ready("krylov", "node_wts", "self_inv", "parent_centers", "up_dirs")
+    begin_interp(0)
+    begin(
+        near_list=(near_list_hbm, near_list), leaf_src=(leaf_src_hbm, leaf_src), leaf_op=(leaf_op_hbm, leaf_op),
+        up_src=(up_src_hbm, up_src), up_op=(up_op_hbm, up_op),
+        up_ops=(up_ops_hbm.at[:, :, pl.ds(pl.multiple_of(member_of_team * part, part), part)], up_ops),
+        leaf_ops=(leaf_ops_hbm, leaf_ops),
+    )
     pairs = []
     for e in range(ells):
         rounded = jnp.concatenate([krylov[q, vectors - 1, e] for q in range(2)], axis=0).astype(BF16)
@@ -319,7 +346,7 @@
 
     for slot, h in enumerate(halves):
         cosine, sine = turns_of(centers, up_dirs[h])
-        for t in range(twins):
+        for t in range(team):
             phases[slot, t, 0] = cosine[:, t * part : (t + 1) * part]
             phases[slot, t, 1] = sine[:, t * part : (t + 1) * part]
 
@@ -336,40 +363,29 @@
     for item in pending:
         gather_up(*item)
 
-    pl.semaphore_wait(barrier, nd - 1)
-    start_a()
     whole = pair(jnp.concatenate([pat[boxes + b] for b in range(boxes)], axis=0))
 
-    def lift(slot):
-        ready(("interp", slot))
-        parents = []
-        for t in range(twins):
-            table = interp_raw[slot, :, t * part : (t + 1) * part].astype(BF16)
-            interp[slot, t] = table
-            lifted = jnp.dot(whole, table, preferred_element_type=F32)
-            lifted = lifted[: boxes * rows] + lifted[boxes * rows :]
-            parent = None
-            for b in range(boxes):
-                piece = lifted[b * rows : (b + 1) * rows]
-                term = outward(
-                    piece * phases[slot, t, 0, b : b + 1, :], piece * phases[slot, t, 1, b : b + 1, :]
-                )
-                parent = term if parent is None else parent + term
-            parents.append(parent)
-        return parents
-
-    for t, parent in enumerate(lift(1)):
-        give[t] = parent
-    partner_id = {"box": bi, "sample": (si + 1) % ns}
-    swap_parts = pltpu.make_async_remote_copy(
-        src_ref=give, dst_ref=take, send_sem=local_sem.at[4], recv_sem=recv_sem.at[0],
-        device_id=partner_id, device_id_type=MESH,
-    )
-    swap_parts.start()
-    own_part = lift(0)
-    swap_parts.wait_recv()
-    for t in range(twins):
-        parents[t] = own_part[t] + take[t]
+    def lift(slot, t):
+        table = interp_raw[slot, :, t * part : (t + 1) * part].astype(BF16)
+        interp[slot, t] = table
+        lifted = jnp.dot(whole, table, preferred_element_type=F32)
+        lifted = lifted[: boxes * rows] + lifted[boxes * rows :]
+        parent = None
+        for b in range(boxes):
+            piece = lifted[b * rows : (b + 1) * rows]
+            term = outward(
+                piece * phases[slot, t, 0, b : b + 1, :], piece * phases[slot, t, 1, b : b + 1, :]
+            )
+            parent = term if parent is None else parent + term
+        return parent
+
+    partner_id = {"box": bi, "sample": cores[1]}
+
+    def swap_part(t):
+        return pltpu.make_async_remote_copy(
+            src_ref=give.at[t], dst_ref=take.at[t], send_sem=local_sem.at[4], recv_sem=recv_sem.at[6 + t],
+            device_id=partner_id, device_id_type=MESH,
+        )
 
     def bulk(ref, send, receive):
         return pltpu.make_async_remote_copy(
@@ -377,22 +393,33 @@
             device_id=partner_id, device_id_type=MESH,
         )
 
-    def deliver(box):
+    def deliver(box, t):
         pltpu.make_async_remote_copy(
-            src_ref=parents.at[box % twins], dst_ref=gathered.at[bi], send_sem=local_sem.at[5],
+            src_ref=parents.at[t], dst_ref=gathered.at[bi], send_sem=local_sem.at[5],
             recv_sem=recv_sem.at[1], device_id={"box": box, "sample": si}, device_id_type=MESH,
         ).start()
 
-    for distance in range(levels - 1, 0, -1):
-        for there, up in ((level + distance < levels, 1), (level >= distance, -1)):
-            @pl.when(there)
-            def _(distance=distance, up=up):
-                for turned in range(twins):
-                    deliver((level + up * distance) * twins + (bi + turned) % twins)
-    if twins > 1:
-        deliver(level * twins + (bi + 1) % twins)
+    ready(("interp", 1))
+    for t in range(team):
+        give[t] = lift(1, t)
+    pl.semaphore_wait(barrier, nd - 1)
+    for t in range(team):
+        swap_part(t).start()
+    start_a()
+    ready(("interp", 0))
+    own_part = [lift(0, t) for t in range(team)]
+    for t in range(team):
+        swap_part(t).wait_recv()
+        parents[t] = own_part[t] + take[t]
+        for base in bases[:-1]:
+            deliver(base + t, t)
+
+        @pl.when(member_of_team != t)
+        def _(t=t):
+            deliver(bases[-1] + t, t)
+
     every_parent = bulk(gathered.at[pl.ds(0, nb - 1)], 5, 1)
-    gathered[bi] = parents[twin]
+    gathered[bi] = parents[member_of_team]
     start_b()
 
     def edge(x, first, ones):
@@ -450,11 +477,16 @@
         values = near_source(e, j)[0:rows]
         near_acc[e] += inward(both(values, near_r[slot], 1), both(values, near_i[slot], 1))
 
-    distances(0)
-    for index in range(pairs_total):
-        if index + 1 < pairs_total:
-            distances(index + 1)
-        near_pair(index)
+    def near_run(start, stop):
+        if start < stop:
+            distances(start)
+        for index in range(start, stop):
+            if index + 1 < stop:
+                distances(index + 1)
+            near_pair(index)
+
+    early = pairs_total - min(LATE, pairs_total)
+    near_run(0, early)
 
     ready("up_src", "up_op", "up_ops")
     every_parent.wait_recv()
@@ -466,22 +498,30 @@
             total = term if total is None else total + term
         return total
 
+    mine = si * team + member_of_team
+    first_box = bi - member_of_team
+    team_levels = team // twins if team > 1 else 1
+
     def hand(source, receive, box, sample):
         pltpu.make_async_remote_copy(
-            src_ref=source, dst_ref=full.at[si, twin], send_sem=local_sem.at[6], recv_sem=recv_sem.at[receive],
+            src_ref=source, dst_ref=full.at[mine], send_sem=local_sem.at[6], recv_sem=recv_sem.at[receive],
             device_id={"box": box, "sample": sample}, device_id_type=MESH,
         ).start()
 
-    other_twin = (twin + 1) % twins
-    handed = 1
-    if twins > 1:
-        other_box = level * twins + other_twin
-        cross[...] = coarse(other_box)
+    def mate(rise, turned):
+        return ((member_of_team // twins + rise) % team_levels) * twins + (member_of_team + turned) % twins
+
+    close = [mate(0, turned) for turned in range(1, twins)] if team > 1 else []
+    distant = [mate(rise, turned) for rise in range(team_levels - 1, 0, -1) for turned in range(twins)]
+    for slot, (to, receive) in enumerate([(to, 5) for to in distant] + [(to, 3) for to in close]):
+        cross[slot] = coarse(first_box + to)
         for off in range(ns - 1, -1, -1):
-            hand(cross, 3, other_box, (si + off) % ns)
-        handed += ns
-    full[si, twin] = coarse(bi)
-    hand(full.at[si, twin], 2, bi, (si + 1) % ns)
+            hand(cross.at[slot], receive, first_box + to, (si + off) % ns)
+    full[mine] = coarse(bi)
+    hand(full.at[mine], 2, bi, (si + 1) % ns)
+    handed = bulk(full.at[pl.ds(0, 1 + ns * (team - 1))], 6, 2)
+
+    near_run(early, pairs_total)
 
     arrive_b()
     ready("leaf_src", "leaf_op", "leaf_ops")
@@ -496,7 +536,7 @@
 
 
     def lower(slot, t):
-        values = full[halves[slot], t]
+        values = full[halves[slot] * team + t]
         lowered = jnp.concatenate(
             [
                 inward(values * phases[slot, t, 0, b : b + 1, :], values * phases[slot, t, 1, b : b + 1, :])
@@ -506,13 +546,15 @@
         )
         return both(lowered, interp[slot, t], 1)
 
-    lowered = lower(0, twin)
-    bulk(cross, 6, 2).wait_recv()
-    lowered = lowered + lower(1, twin)
-    if twins > 1:
-        bulk(gathered.at[pl.ds(0, ns)], 6, 3).wait_recv()
-        for slot in range(ns):
-            lowered = lowered + lower(slot, other_twin)
+    lowered = lower(0, member_of_team)
+    bulk(full.at[0], 6, 2).wait_recv()
+    lowered = lowered + lower(1, member_of_team)
+    for mates, receive in ((close, 3), (distant, 5)):
+        if mates:
+            bulk(full.at[pl.ds(0, ns * len(mates))], 6, receive).wait_recv()
+        for t in mates:
+            for slot in range(ns):
+                lowered = lowered + lower(slot, t)
     for b in range(boxes):
         incoming[b] = incoming[b] + lowered[b * rows : (b + 1) * rows]
 
@@ -540,28 +582,43 @@
         b = jnp.broadcast_to(crossed[m], lane.shape)
         dots = jnp.where(row < inc, a + swap(a), swap(b) - b)
         packed = packed + jnp.where(lane == m * rows + row, dots, 0.0)
-    sums[dev] = jnp.sum(packed, axis=0, keepdims=True)
+    share_row[...] = jnp.sum(packed, axis=0, keepdims=True)
+
     def share(box, sample):
         pltpu.make_async_remote_copy(
-            src_ref=sums.at[dev], dst_ref=sums.at[dev], send_sem=local_sem.at[7], recv_sem=recv_sem.at[4],
+            src_ref=share_row, dst_ref=sums_hbm.at[dev], send_sem=local_sem.at[7], recv_sem=recv_sem.at[4],
             device_id={"box": box, "sample": sample}, device_id_type=MESH,
         ).start()
 
-    for distance in range(levels - 1, 0, -1):
-        for there, up in ((level + distance < levels, 1), (level >= distance, -1)):
-            @pl.when(there)
-            def _(distance=distance, up=up):
-                for turned in range(twins):
-                    for flip in range(ns):
-                        share((level + up * distance) * twins + (bi + turned) % twins, (si + flip) % ns)
-    for near in range(twins * ns - 1, 0, -1):
-        share(level * twins + (bi + near // ns) % twins, (si + near % ns) % ns)
-    every_sum = bulk(sums.at[pl.ds(0, nd - 1)], 7, 4)
+    all_others(share)
+    outs = [
+        pltpu.make_async_copy(share_row, sums_hbm.at[dev], local_sem.at[8]),
+        pltpu.make_async_copy(result, result_hbm, local_sem.at[9]),
+    ]
+    for copy in outs:
+        copy.start()
+    finish_a()
+    finish_b()
+    handed.wait_send()
+    bulk(full.at[pl.ds(0, team)], 4, 0).wait_send()
+    every_parent.wait_send()
+    every_sum = bulk(sums_hbm.at[pl.ds(0, nd - 1)], 7, 4)
+    every_sum.wait_send()
+    for copy in outs:
+        copy.wait()
     every_sum.wait_recv()
+
+
+def finish(sums, result, krylov, h_out, norm_out, next_out):
+    _, vectors, ells, inc, nodes = krylov.shape
+    rows = 2 * inc
+    lane = lax.broadcasted_iota(jnp.int32, (rows, 128), 1)
+    row = lax.broadcasted_iota(jnp.int32, (rows, 128), 0)
+    sign = jnp.where(lax.broadcasted_iota(jnp.int32, (rows, 1), 0) < inc, 1.0, -1.0)
     total = sums[0]
-    for index in range(1, nd):
+    for index in range(1, sums.shape[0]):
         total = total + sums[index]
-    total = total * (1.0 / (ells * nodes * nd))
+    total = total * (1.0 / (ells * nodes * sums.shape[0]))
     spread = jnp.broadcast_to(total, lane.shape)
 
     def column(start):
@@ -578,42 +635,19 @@
     for m in range(vectors):
         for q in range(2):
             at = m * rows + q * inc
-            small_out[q * vectors + m : q * vectors + m + 1, 0:inc] = total[:, at : at + inc]
+            h_out[q, m : m + 1, :] = total[:, at : at + inc]
     flat = jnp.sum(
         jnp.where((lane == row) & (row < inc), jnp.broadcast_to(norm, lane.shape), 0.0), axis=0, keepdims=True
     )
-    small_out[2 * vectors : 2 * vectors + 1, :] = flat
+    norm_out[...] = flat[:, 0:inc]
     for e in range(ells):
         kept = result[e]
         for m in range(vectors):
-            basis = ks[m, e]
-            kept = kept - inward(basis * real[m], basis * imag[m])
+            basis = jnp.concatenate([krylov[q, m, e] for q in range(2)], axis=0)
+            kept = kept - (basis * real[m] - sign * pltpu.roll(basis * imag[m], inc, 0))
         kept = kept / norm
         for q in range(2):
             next_out[q, e] = kept[q * inc : (q + 1) * inc]
-    outs = [
-        pltpu.make_async_copy(next_out, next_hbm, local_sem.at[8]),
-        pltpu.make_async_copy(small_out, small_hbm, local_sem.at[9]),
-    ]
-    for copy in outs:
-        copy.start()
-
-    finish_a()
-    finish_b()
-    bulk(gathered.at[pl.ds(0, handed)], 6, 2).wait_send()
-    swap_parts.wait_send()
-    every_parent.wait_send()
-    every_sum.wait_send()
-    for copy in outs:
-        copy.wait()
-
-
-def hand_on(small_in, next_in, h_out, norm_out, next_out):
-    _, vectors, inc = h_out.shape
-    next_out[...] = next_in[...]
-    for q in range(2):
-        h_out[q] = small_in[q * vectors : (q + 1) * vectors, 0:inc]
-    norm_out[...] = small_in[2 * vectors : 2 * vectors + 1, 0:inc]
 
 
 def body(
@@ -640,8 +674,8 @@
     leaf_width, up_width = interp.shape
     half = up_ops.shape[2]
     nd = nb * ns
-    twins = 2 if nb % 2 == 0 else 1
-    part = half // twins
+    team = next(size for size in (TEAM, 2, 1) if nb % size == 0)
+    part = half // team
     directions = sphere_points(leaf_width).T
     pieces = []
     for _ in range(3):
@@ -663,10 +697,12 @@
         jax.ShapeDtypeStruct((1, inc), F32),
         jax.ShapeDtypeStruct((2, ells, inc, nodes), F32),
     )
-    small_shape = jax.ShapeDtypeStruct((16 * ((2 * vectors + 16) // 16), 128), F32)
-    small_rows, next_rows = pl.pallas_call(
+    sums, result = pl.pallas_call(
         functools.partial(kernel, nb, ns),
-        out_shape=(small_shape, shapes[2]),
+        out_shape=(
+            jax.ShapeDtypeStruct((nd, 1, 128), F32),
+            jax.ShapeDtypeStruct((ells, rows, nodes), F32),
+        ),
         in_specs=[hbm] * 16,
         out_specs=(hbm, hbm),
         scratch_shapes=[pltpu.SMEM(x.shape, x.dtype) for x in small]
@@ -675,45 +711,43 @@
             pltpu.VMEM(leaf_ops.shape, F32),
             pltpu.VMEM((ns, leaf_width, half), F32),
             pltpu.VMEM((*up_ops.shape[:2], part), F32),
-            pltpu.VMEM((ns, twins, leaf_width, part), BF16),
+            pltpu.VMEM((ns, team, leaf_width, part), BF16),
             pltpu.VMEM((vectors, ells, rows, nodes), F32),
             pltpu.VMEM((3 * ells, rows + 8, nodes), F32),
-            pltpu.VMEM((ns, twins, 2, boxes, part), F32),
+            pltpu.VMEM((ns, team, 2, boxes, part), F32),
             pltpu.VMEM((ells, nodes, 8 * len(SPLITS) + 16), BF16),
             pltpu.VMEM((ells, 8 * len(SPLITS), nodes), BF16),
             pltpu.VMEM((ells, leaf_width, nodes), F32),
             pltpu.VMEM((ells, leaf_width, nodes), BF16),
             pltpu.VMEM((ells, leaf_width, nodes), BF16),
             pltpu.VMEM((3 * boxes, rows, leaf_width), F32),
-            pltpu.VMEM((twins, rows, part), F32),
-            pltpu.VMEM((twins, rows, part), F32),
-            pltpu.VMEM((twins, rows, part), F32),
+            pltpu.VMEM((team, rows, part), F32),
+            pltpu.VMEM((team, rows, part), F32),
+            pltpu.VMEM((team, rows, part), F32),
             pltpu.VMEM((nb, rows, part), F32),
-            pltpu.VMEM((rows, part), F32),
-            pltpu.VMEM((ns, twins, rows, part), F32),
+            pltpu.VMEM((team, rows, part), F32),
+            pltpu.VMEM((ns * team, rows, part), F32),
             pltpu.VMEM((2, nodes, nodes), F32),
             pltpu.VMEM((2, nodes, nodes), BF16),
             pltpu.VMEM((2, nodes, nodes), BF16),
             pltpu.VMEM((ells, rows, nodes), F32),
             pltpu.VMEM((ells, rows, nodes), F32),
-            pltpu.VMEM((nd, 1, 128), F32),
+            pltpu.VMEM((1, 128), F32),
             dma((ns + 15,)),
             dma((2,)),
             dma((2,)),
-            dma((5,)),
-            pltpu.VMEM(small_shape.shape, F32),
-            pltpu.VMEM(shapes[2].shape, F32),
+            dma((6 + team,)),
         ],
         compiler_params=pltpu.CompilerParams(
             collective_id=0, has_side_effects=True, vmem_limit_bytes=67043328
         ),
     )(*small, *large, leaf_ops, interp, up_ops)
     h_column, h_norm, next_vector = pl.pallas_call(
-        hand_on,
+        finish,
         out_shape=shapes,
-        in_specs=[vmem] * 2,
+        in_specs=[vmem] * 3,
         out_specs=(vmem, vmem, vmem),
-    )(small_rows, next_rows)
+    )(sums, result, large[0])
     return h_column, h_norm.reshape(inc), jnp.transpose(next_vector, (0, 2, 1, 3))
 
 

time: 23.3 us -> 21.7 us (0.931)
  Pallas kernels: 22.4 us -> 20.9 us
    pallas_call x2, Pallas kernels: 22.4 us -> 20.9 us  [the longest x1 19.2 us: body(): pl.pallas_call(functools.partial(kernel, nb, ns), out_shape=(jax.ShapeDty...]
where the time goes in v3:
time: 21.7 us; the launch traced here: 21.5 us
  Pallas kernels  20.9 us (96%)
  between operations  0.64 us (3%)
    pallas_call x1, Pallas kernels, body(): pl.pallas_call(functools.partial(kernel, nb, ns), out_shape=(jax.ShapeDty...  19.2 us
    pallas_call x1, Pallas kernels, body(): pl.pallas_call(finish, out_shape=shapes, in_specs=[vmem] * 3, out_specs=(...  1.69 us

profile of v3, /device:TPU:0, one launch (start us, length us, event | category | flops | bytes accessed | tf_op | source)
XLA Modules:
  0.0 21.5 jit_solution(10766634119749672812)
XLA Ops:
  0.6 19.2 %shard_map.175 = (f32[16,1,128]{2,1,0:T(1,128)}, f32[3,8,256]{2,1,0:T(8,128)}) custom-call(s32[3]{0:T(128)} %box_of_hbm.1, s32[3,4]{1,0:T(4,128)} %near_list_hbm.1, s32[2,4]{1,0:T(2,128)} %leaf_src_hbm.1, s32[2,4]{1,0:T(2,128)} %leaf_op_hbm.1, s32[8,6]{1,0:T(8,128)} %up_src_hbm.1, s32[8,6]{1,0:T(8,128)} %up_op_hbm.1, f32[1,3]{1,0:T(1,128)} %bitcast.6, ...), custom_call_target="tpu_custom_call" | custom-call | tf_op jit(solution)/shard_map/pallas_call | solution.py:700
  19.8 1.7 %shard_map.176 = (f32[2,4,4]{2,1,0:T(4,128)}, f32[1,4]{1,0:T(1,128)}, f32[2,3,4,256]{3,2,1,0:T(4,128)}) custom-call(f32[16,1,128]{2,1,0:T(1,128)} %get-tuple-element.8.sums, f32[3,8,256]{2,1,0:T(8,128)} %get-tuple-element.9.result, f32[2,4,3,4,256]{4,3,2,1,0:T(4,128)} %bitcast.5), custom_call_target="tpu_custom_call" | custom-call | tf_op jit(solution)/shard_map/pallas_call | solution.py:745

commit v4 on v3

--- a/solution.py
+++ b/solution.py
@@ -168,9 +168,9 @@
 
     loads = {}
 
-    def begin(**arrays):
-        for name, (source, target) in arrays.items():
-            loads[name] = load(len(loads), source, target)
+    def begin(first, **arrays):
+        for slot, (name, (source, target)) in enumerate(arrays.items()):
+            loads[name] = load(first + slot, source, target)
 
     def ready(*wanted):
         for name in wanted:
@@ -179,11 +179,14 @@
     def place(index):
         return {"box": index // ns, "sample": index % ns}
 
-    begin(box_of=(box_of_hbm, box_of), node_pos=(node_pos_hbm, node_pos), leaf_dirs=(leaf_dirs_hbm, leaf_dirs))
+    begin(0, box_of=(box_of_hbm, box_of), node_pos=(node_pos_hbm, node_pos), leaf_dirs=(leaf_dirs_hbm, leaf_dirs))
     barrier = pltpu.get_barrier_semaphore()
+    shift = 0
+    far_first = [wrapped(t + shift, team) for t in range(team)]
+
     def all_others(act):
         for base in bases[:-1]:
-            for t in range(team):
+            for t in far_first:
                 for core in cores:
                     act(base + t, core)
         for turn_by in range(team):
@@ -196,14 +199,14 @@
         )
     )
     begin(
-        krylov=(krylov_hbm, krylov), node_wts=(node_wts_hbm, node_wts), self_inv=(self_inv_hbm, self_inv),
+        3, krylov=(krylov_hbm, krylov), node_wts=(node_wts_hbm, node_wts), self_inv=(self_inv_hbm, self_inv),
         parent_centers=(parent_centers_hbm, parent_centers), up_dirs=(up_dirs_hbm, up_dirs),
     )
     halves = cores[:2]
 
     def begin_interp(slot):
         at = pl.ds(pl.multiple_of(halves[slot] * half, half), half)
-        loads["interp", slot] = load(len(loads), interp_hbm.at[:, at], interp_raw.at[slot])
+        loads["interp", slot] = load(9 - slot, interp_hbm.at[:, at], interp_raw.at[slot])
 
     begin_interp(1)
 
@@ -230,11 +233,15 @@
         )
 
         def start():
+            @pl.when((si == 0) & (dev > 0))
+            def _():
+                left.start()
+
             @pl.when(dev < nd - 1)
             def _():
                 right.start()
 
-            @pl.when(dev > 0)
+            @pl.when(si > 0)
             def _():
                 left.start()
 
@@ -258,8 +265,8 @@
 
         return start, arrive, finish
 
-    start_a, arrive_a, finish_a = neighbours(halo, ells, 0, recv_a)
-    start_b, arrive_b, finish_b = neighbours(pat, boxes, 2, recv_b)
+    start_a, arrive_a, finish_a = neighbours(halo, ells, 7, recv_a)
+    start_b, arrive_b, finish_b = neighbours(pat, boxes, 7, recv_b)
 
     ready("node_pos", "box_of")
     for e in range(ells):
@@ -319,7 +326,7 @@
     ready("krylov", "node_wts", "self_inv", "parent_centers", "up_dirs")
     begin_interp(0)
     begin(
-        near_list=(near_list_hbm, near_list), leaf_src=(leaf_src_hbm, leaf_src), leaf_op=(leaf_op_hbm, leaf_op),
+        0, near_list=(near_list_hbm, near_list), leaf_src=(leaf_src_hbm, leaf_src), leaf_op=(leaf_op_hbm, leaf_op),
         up_src=(up_src_hbm, up_src), up_op=(up_op_hbm, up_op),
         up_ops=(up_ops_hbm.at[:, :, pl.ds(pl.multiple_of(member_of_team * part, part), part)], up_ops),
         leaf_ops=(leaf_ops_hbm, leaf_ops),
@@ -383,7 +390,7 @@
 
     def swap_part(t):
         return pltpu.make_async_remote_copy(
-            src_ref=give.at[t], dst_ref=take.at[t], send_sem=local_sem.at[4], recv_sem=recv_sem.at[6 + t],
+            src_ref=give.at[t], dst_ref=take.at[t], send_sem=local_sem.at[10], recv_sem=recv_sem.at[0],
             device_id=partner_id, device_id_type=MESH,
         )
 
@@ -395,7 +402,7 @@
 
     def deliver(box, t):
         pltpu.make_async_remote_copy(
-            src_ref=parents.at[t], dst_ref=gathered.at[bi], send_sem=local_sem.at[5],
+            src_ref=parents.at[t], dst_ref=gathered.at[bi], send_sem=local_sem.at[9],
             recv_sem=recv_sem.at[1], device_id={"box": box, "sample": si}, device_id_type=MESH,
         ).start()
 
@@ -408,9 +415,11 @@
     start_a()
     ready(("interp", 0))
     own_part = [lift(0, t) for t in range(team)]
+    swapped = bulk(full.at[pl.ds(0, team)], 10, 0)
+    swapped.wait_recv()
     for t in range(team):
-        swap_part(t).wait_recv()
         parents[t] = own_part[t] + take[t]
+    for t in range(team):
         for base in bases[:-1]:
             deliver(base + t, t)
 
@@ -418,8 +427,10 @@
         def _(t=t):
             deliver(bases[-1] + t, t)
 
-    every_parent = bulk(gathered.at[pl.ds(0, nb - 1)], 5, 1)
+    every_parent = bulk(gathered.at[pl.ds(0, nb - 1)], 9, 1)
     gathered[bi] = parents[member_of_team]
+    swapped.wait_send()
+    finish_a()
     start_b()
 
     def edge(x, first, ones):
@@ -504,7 +515,7 @@
 
     def hand(source, receive, box, sample):
         pltpu.make_async_remote_copy(
-            src_ref=source, dst_ref=full.at[mine], send_sem=local_sem.at[6], recv_sem=recv_sem.at[receive],
+            src_ref=source, dst_ref=full.at[mine], send_sem=local_sem.at[0], recv_sem=recv_sem.at[receive],
             device_id={"box": box, "sample": sample}, device_id_type=MESH,
         ).start()
 
@@ -519,7 +530,7 @@
             hand(cross.at[slot], receive, first_box + to, (si + off) % ns)
     full[mine] = coarse(bi)
     hand(full.at[mine], 2, bi, (si + 1) % ns)
-    handed = bulk(full.at[pl.ds(0, 1 + ns * (team - 1))], 6, 2)
+    handed = bulk(full.at[pl.ds(0, 1 + ns * (team - 1))], 0, 2)
 
     near_run(early, pairs_total)
 
@@ -547,11 +558,11 @@
         return both(lowered, interp[slot, t], 1)
 
     lowered = lower(0, member_of_team)
-    bulk(full.at[0], 6, 2).wait_recv()
+    bulk(full.at[0], 0, 2).wait_recv()
     lowered = lowered + lower(1, member_of_team)
     for mates, receive in ((close, 3), (distant, 5)):
         if mates:
-            bulk(full.at[pl.ds(0, ns * len(mates))], 6, receive).wait_recv()
+            bulk(full.at[pl.ds(0, ns * len(mates))], 0, receive).wait_recv()
         for t in mates:
             for slot in range(ns):
                 lowered = lowered + lower(slot, t)
@@ -586,23 +597,21 @@
 
     def share(box, sample):
         pltpu.make_async_remote_copy(
-            src_ref=share_row, dst_ref=sums_hbm.at[dev], send_sem=local_sem.at[7], recv_sem=recv_sem.at[4],
+            src_ref=share_row, dst_ref=sums_hbm.at[dev], send_sem=local_sem.at[10], recv_sem=recv_sem.at[4],
             device_id={"box": box, "sample": sample}, device_id_type=MESH,
         ).start()
 
     all_others(share)
     outs = [
-        pltpu.make_async_copy(share_row, sums_hbm.at[dev], local_sem.at[8]),
-        pltpu.make_async_copy(result, result_hbm, local_sem.at[9]),
+        pltpu.make_async_copy(share_row, sums_hbm.at[dev], local_sem.at[1]),
+        pltpu.make_async_copy(result, result_hbm, local_sem.at[2]),
     ]
     for copy in outs:
         copy.start()
-    finish_a()
     finish_b()
     handed.wait_send()
-    bulk(full.at[pl.ds(0, team)], 4, 0).wait_send()
     every_parent.wait_send()
-    every_sum = bulk(sums_hbm.at[pl.ds(0, nd - 1)], 7, 4)
+    every_sum = bulk(sums_hbm.at[pl.ds(0, nd - 1)], 10, 4)
     every_sum.wait_send()
     for copy in outs:
         copy.wait()
@@ -733,10 +742,10 @@
             pltpu.VMEM((ells, rows, nodes), F32),
             pltpu.VMEM((ells, rows, nodes), F32),
             pltpu.VMEM((1, 128), F32),
-            dma((ns + 15,)),
+            dma((11,)),
             dma((2,)),
             dma((2,)),
-            dma((6 + team,)),
+            dma((6,)),
         ],
         compiler_params=pltpu.CompilerParams(
             collective_id=0, has_side_effects=True, vmem_limit_bytes=67043328

time: 21.7 us -> 21.6 us (level)
  no operation moved by 1% of the time
where the time goes in v4:
time: 21.6 us; the launch traced here: 21.4 us
  Pallas kernels  20.8 us (96%)
  between operations  0.64 us (3%)
    pallas_call x1, Pallas kernels, body(): pl.pallas_call(functools.partial(kernel, nb, ns), out_shape=(jax.ShapeDty...  19.1 us
    pallas_call x1, Pallas kernels, body(): pl.pallas_call(finish, out_shape=shapes, in_specs=[vmem] * 3, out_specs=(...  1.69 us

profile of v4, /device:TPU:0, one launch (start us, length us, event | category | flops | bytes accessed | tf_op | source)
XLA Modules:
  0.0 21.4 jit_solution(7615399384686283280)
XLA Ops:
  0.6 19.1 %shard_map.175 = (f32[16,1,128]{2,1,0:T(1,128)}, f32[3,8,256]{2,1,0:T(8,128)}) custom-call(s32[3]{0:T(128)} %box_of_hbm.1, s32[3,4]{1,0:T(4,128)} %near_list_hbm.1, s32[2,4]{1,0:T(2,128)} %leaf_src_hbm.1, s32[2,4]{1,0:T(2,128)} %leaf_op_hbm.1, s32[8,6]{1,0:T(8,128)} %up_src_hbm.1, s32[8,6]{1,0:T(8,128)} %up_op_hbm.1, f32[1,3]{1,0:T(1,128)} %bitcast.6, ...), custom_call_target="tpu_custom_call" | custom-call | tf_op jit(solution)/shard_map/pallas_call | solution.py:709
  19.8 1.7 %shard_map.176 = (f32[2,4,4]{2,1,0:T(4,128)}, f32[1,4]{1,0:T(1,128)}, f32[2,3,4,256]{3,2,1,0:T(4,128)}) custom-call(f32[16,1,128]{2,1,0:T(1,128)} %get-tuple-element.8.sums, f32[3,8,256]{2,1,0:T(8,128)} %get-tuple-element.9.result, f32[2,4,3,4,256]{4,3,2,1,0:T(4,128)} %bitcast.5), custom_call_target="tpu_custom_call" | custom-call | tf_op jit(solution)/shard_map/pallas_call | solution.py:754

commit v5 on v4

--- a/solution.py
+++ b/solution.py
@@ -13,7 +13,7 @@
 F32 = jnp.float32
 BF16 = jnp.bfloat16
 ROWS = 64
-SPAN = 128
+SPAN = 256
 TEAM = 4
 LATE = 8
 SPLITS = ((0, 0), (1, 0), (2, 0), (0, 1), (1, 1), (0, 2))
@@ -415,24 +415,6 @@
     start_a()
     ready(("interp", 0))
     own_part = [lift(0, t) for t in range(team)]
-    swapped = bulk(full.at[pl.ds(0, team)], 10, 0)
-    swapped.wait_recv()
-    for t in range(team):
-        parents[t] = own_part[t] + take[t]
-    for t in range(team):
-        for base in bases[:-1]:
-            deliver(base + t, t)
-
-        @pl.when(member_of_team != t)
-        def _(t=t):
-            deliver(bases[-1] + t, t)
-
-    every_parent = bulk(gathered.at[pl.ds(0, nb - 1)], 9, 1)
-    gathered[bi] = parents[member_of_team]
-    swapped.wait_send()
-    finish_a()
-    start_b()
-
     def edge(x, first, ones):
         parts = thirds(jnp.sum(x * x, axis=0, keepdims=True))
         at = lax.broadcasted_iota(jnp.int32, x.shape, 0)
@@ -450,6 +432,24 @@
         for m in range(vectors):
             for q in range(2):
                 ks[m, e, q * inc : (q + 1) * inc, :] = krylov[q, m, e]
+
+    swapped = bulk(full.at[pl.ds(0, team)], 10, 0)
+    swapped.wait_recv()
+    for t in range(team):
+        parents[t] = own_part[t] + take[t]
+    for t in range(team):
+        for base in bases[:-1]:
+            deliver(base + t, t)
+
+        @pl.when(member_of_team != t)
+        def _(t=t):
+            deliver(bases[-1] + t, t)
+
+    every_parent = bulk(gathered.at[pl.ds(0, nb - 1)], 9, 1)
+    gathered[bi] = parents[member_of_team]
+    swapped.wait_send()
+    finish_a()
+    start_b()
 
     def translate(operators, index, values):
         pair_rows = operators[index]

time: 21.6 us -> 21.6 us (level)
  no operation moved by 1% of the time
where the time goes in v5:
time: 21.6 us; the launch traced here: 21.4 us
  Pallas kernels  20.8 us (96%)
  between operations  0.64 us (3%)
    pallas_call x1, Pallas kernels, body(): pl.pallas_call(functools.partial(kernel, nb, ns), out_shape=(jax.ShapeDty...  19.1 us
    pallas_call x1, Pallas kernels, body(): pl.pallas_call(finish, out_shape=shapes, in_specs=[vmem] * 3, out_specs=(...  1.69 us

profile of v5, /device:TPU:0, one launch (start us, length us, event | category | flops | bytes accessed | tf_op | source)
XLA Modules:
  0.0 21.4 jit_solution(14761581404321724117)
XLA Ops:
  0.6 19.1 %shard_map.175 = (f32[16,1,128]{2,1,0:T(1,128)}, f32[3,8,256]{2,1,0:T(8,128)}) custom-call(s32[3]{0:T(128)} %box_of_hbm.1, s32[3,4]{1,0:T(4,128)} %near_list_hbm.1, s32[2,4]{1,0:T(2,128)} %leaf_src_hbm.1, s32[2,4]{1,0:T(2,128)} %leaf_op_hbm.1, s32[8,6]{1,0:T(8,128)} %up_src_hbm.1, s32[8,6]{1,0:T(8,128)} %up_op_hbm.1, f32[1,3]{1,0:T(1,128)} %bitcast.6, ...), custom_call_target="tpu_custom_call" | custom-call | tf_op jit(solution)/shard_map/pallas_call | solution.py:709
  19.7 1.7 %shard_map.176 = (f32[2,4,4]{2,1,0:T(4,128)}, f32[1,4]{1,0:T(1,128)}, f32[2,3,4,256]{3,2,1,0:T(4,128)}) custom-call(f32[16,1,128]{2,1,0:T(1,128)} %get-tuple-element.8.sums, f32[3,8,256]{2,1,0:T(8,128)} %get-tuple-element.9.result, f32[2,4,3,4,256]{4,3,2,1,0:T(4,128)} %bitcast.5), custom_call_target="tpu_custom_call" | custom-call | tf_op jit(solution)/shard_map/pallas_call | solution.py:754
